TPU v7x, 128 devices: a whole 4x4x4 slice. The times are simulated.
128 devices in a mesh: zone: 32 (over y, x, core), sub: 4 (over z).
Axes of the slice: x: 4, y: 4, z: 4, core: 2. Of those that a mesh axis runs over, the one named last changes fastest.
Arguments:
- order_features: bfloat16 [262144, 128], P('zone'), may hold values from -6 to 6
- w_in: bfloat16 [128, 512], replicated, may hold values from -0.5 to 0.5
- bias_in: float32 [512], replicated, may hold values from -3 to 3
- w_out: bfloat16 [512, 128], replicated, may hold values from -0.25 to 0.25
- bias_out: float32 [128], replicated, may hold values from -3 to 3
- courier_embed: bfloat16 [65536, 128], P(('zone', 'sub')), may hold values from -28 to 28
- courier_cap: bfloat16 [65536], P(('zone', 'sub')), may hold values from 0.5 to 4
- adjacency: int32 [512, 8], P('zone'), may hold values from 0 to 127, all different within a row; in each aligned block of 16 rows (0 to 15, 16 to 31, ...) at most 2 rows name the same one
- order_count: int32 [512], P('zone'), may hold values from 64 to 512
- courier_count: int32 [128], P(('zone', 'sub')), may hold values from 64 to 512
Outputs:
- order_potentials: float32 [262144], P('zone')
- courier_potentials: float32 [65536], P(('zone', 'sub'))
Inputs may be any that keep to these rules, and one draw needn't show every extreme that they name: `adjacency`: each row names 8 different courier blocks and every courier block is named by some row. Among the 16 rows of one index of zone (aligned blocks of rows), no courier block is named by more than 2 rows, and in some of them one is named by exactly 2.
All inputs are finite; a program needn't handle non-finite values.
Results may differ from a plain program's by a relative error of at most 0.0017.
Values may be sent and summed in bfloat16 or wider, within the bound.
No kernel may reach another device: no remote copies, remote signals or barrier semaphores. Data moves between devices by JAX's collectives and lax.ppermute only.
A program may use at most 128 MiB of HBM per device.

v0:
```python
import math

import jax
import jax.numpy as jnp
from jax import lax
from jax.experimental import pallas as pl
from jax.experimental.pallas import tpu as pltpu
from jax.sharding import PartitionSpec as P

BLOCK = 512
EMB = 128
HID = 512
ADJ = 8
OB_DEV = 16
ZONES = 32
SUBS = 4
HALF = 256
COURIER_ROWS = BLOCK + 16
UNROLL = 32
REST = 8
MOST_ENTRIES = 256
LIST_SIZE = MOST_ENTRIES + 2 * REST
NO_ORDER = 2 * OB_DEV
NO_COURIER = 2 * ZONES

TEMPER = 0.2
LOWEST = -1e30
SCORE_SCALE = math.log2(math.e) / (TEMPER * math.sqrt(EMB))
DUAL_SCALE = TEMPER * math.log(2.0)

VMEM_LIMIT = 16 * 1024 * 1024


def zone_of(y, x, core):
    return ((y % 4) * 4 + (x % 4)) * 2 + core


PLACES = [(y, x, core) for y in range(4) for x in range(4) for core in range(2)]


def other_core(value):
    return lax.ppermute(value, "zone", [(zone_of(y, x, c), zone_of(y, x, 1 - c)) for y, x, c in PLACES])


def along_z(value, step):
    return lax.ppermute(value, "sub", [(i, (i + step) % SUBS) for i in range(SUBS)])


def plane_step(value, stage, step):
    pairs = []
    for y, x, c in PLACES:
        to = (y, x + step, c) if stage == c else (y + step, x, c)
        pairs.append((zone_of(y, x, c), zone_of(*to)))
    return lax.ppermute(value, "zone", pairs)


def pack_kernel(count_ref, embed_ref, cap_hbm, block_ref, row_ref, cap_ref, sem):
    copy = pltpu.make_async_copy(embed_ref, block_ref.at[pl.ds(0, BLOCK), :], sem.at[0])
    copy_row = pltpu.make_async_copy(embed_ref, row_ref.at[pl.ds(0, BLOCK), :], sem.at[1])
    copy.start()
    copy_row.start()
    copy_cap = pltpu.make_async_copy(cap_hbm, cap_ref, sem.at[2])
    copy_cap.start()
    copy_cap.wait()
    lane = lax.broadcasted_iota(jnp.int32, (1, BLOCK), 1)
    cap = jnp.where(lane < count_ref[0], cap_ref[...].astype(jnp.float32).reshape(1, BLOCK), 0.0)
    rows = [cap[:, i * EMB : (i + 1) * EMB] for i in range(4)]
    tail = jnp.concatenate(rows + [jnp.zeros((12, EMB), jnp.float32)], axis=0).astype(jnp.bfloat16)
    block_ref[pl.ds(BLOCK, 16), :] = tail
    row_ref[pl.ds(BLOCK, 16), :] = tail
    copy.wait()
    copy_row.wait()


def pack(count, embed, cap):
    vmem = pl.BlockSpec(memory_space=pltpu.VMEM)
    return pl.pallas_call(
        pack_kernel,
        out_shape=(
            jax.ShapeDtypeStruct((COURIER_ROWS, EMB), jnp.bfloat16),
            jax.ShapeDtypeStruct((4 * COURIER_ROWS, EMB), jnp.bfloat16),
        ),
        in_specs=[pl.BlockSpec(memory_space=pltpu.SMEM)] + [pl.BlockSpec(memory_space=pltpu.HBM)] * 2,
        out_specs=(vmem, vmem),
        scratch_shapes=[pltpu.VMEM((BLOCK,), cap.dtype), pltpu.SemaphoreType.DMA((3,))],
        compiler_params=pltpu.CompilerParams(vmem_limit_bytes=4 * 1024 * 1024),
        name="pack",
    )(count, *[pltpu.with_memory_space_constraint(value, pltpu.HBM) for value in (embed, cap)])


def gather_row(block, row):
    for step in (1, 2, 3):
        row = lax.dynamic_update_slice(row, plane_step(block, 0, step), (step * COURIER_ROWS, 0))
    return row


PARTS = 8
EARLY = (0, 4)


def slot_of(zone, me):
    back_x = ((me >> 1) - (zone >> 1)) & 3
    back_y = ((me >> 3) - (zone >> 3)) & 3
    odd = zone & 1
    first = jnp.where(odd == 0, back_x, back_y)
    second = jnp.where(odd == 0, back_y, back_x)
    return ((me ^ zone) & 1) * 16 + second * 4 + first


def early_slot(slot):
    part = slot >> 2
    index = sum(jnp.where(part == p, i, 0) for i, p in enumerate(EARLY))
    is_early = sum(jnp.where(part == p, 1, 0) for p in EARLY)
    return is_early, index * 4 + (slot & 3)


def join(*parts):
    highest = parts[0]
    for part in parts[1:]:
        highest = jnp.maximum(highest, part)
    total = jnp.exp2(parts[0] - highest)
    for part in parts[1:]:
        total = total + jnp.exp2(part - highest)
    return highest + jnp.log2(total)


def join_subs(value):
    return join(value, along_z(value, 1), along_z(value, 2), along_z(value, 3))


def join_zones(value):
    value = join(value, other_core(value))
    for stage in range(2):
        value = join(value, *[plane_step(value, stage, step) for step in (1, 2, 3)])
    return value


EMBED_ROWS = 4096


def embed_kernel(x_hbm, w_in_hbm, b_in_hbm, w_out_hbm, b_out_hbm, o_ref, x_ref, w_in_ref, b_in_ref, w_out_ref, b_out_ref, sem):
    steps = x_ref.shape[0] // EMBED_ROWS

    def rows_copy(i):
        rows = pl.ds(pl.multiple_of(i * EMBED_ROWS, EMBED_ROWS), EMBED_ROWS)
        return pltpu.make_async_copy(x_hbm.at[rows, :], x_ref.at[rows, :], sem.at[i])

    parameters = [
        pltpu.make_async_copy(source, target, sem.at[steps + i])
        for i, (source, target) in enumerate(
            [(w_in_hbm, w_in_ref), (b_in_hbm, b_in_ref), (w_out_hbm, w_out_ref), (b_out_hbm, b_out_ref)]
        )
    ]
    for copy in parameters:
        copy.start()
    for i in range(steps):
        rows_copy(i).start()
    for copy in parameters:
        copy.wait()

    def one_step(i, carry):
        rows_copy(i).wait()
        for start in range(0, EMBED_ROWS, BLOCK):
            rows = pl.ds(pl.multiple_of(i * EMBED_ROWS + start, BLOCK), BLOCK)
            v = jnp.dot(x_ref[rows, :], w_in_ref[...], preferred_element_type=jnp.float32)
            v = 0.5 * (v + b_in_ref[...])
            hidden = (v + v * jnp.tanh(v)).astype(jnp.bfloat16)
            out = jnp.dot(hidden, w_out_ref[...], preferred_element_type=jnp.float32)
            o_ref[rows, :] = ((out + b_out_ref[...]) * SCORE_SCALE).astype(jnp.bfloat16)
        return carry

    lax.fori_loop(0, steps, one_step, 0)


def embed_orders(features, w_in, bias_in, w_out, bias_out):
    rows = features.shape[0]
    operands = (features, w_in, bias_in.reshape(1, HID), w_out, bias_out.reshape(1, EMB))
    return pl.pallas_call(
        embed_kernel,
        out_shape=jax.ShapeDtypeStruct((rows, EMB), jnp.bfloat16),
        in_specs=[pl.BlockSpec(memory_space=pltpu.HBM)] * len(operands),
        out_specs=pl.BlockSpec(memory_space=pltpu.VMEM),
        scratch_shapes=[pltpu.VMEM(value.shape, value.dtype) for value in operands]
        + [pltpu.SemaphoreType.DMA((rows // EMBED_ROWS + 4,))],
        compiler_params=pltpu.CompilerParams(vmem_limit_bytes=VMEM_LIMIT),
        cost_estimate=pl.CostEstimate(
            flops=4 * rows * EMB * HID, bytes_accessed=4 * rows * EMB, transcendentals=rows * HID
        ),
        name="embed_orders",
    )(*[pltpu.with_memory_space_constraint(value, pltpu.HBM) for value in operands])


def list_kernel(pair_ref, two_ref, list_ref, rounds_ref):
    def one_pair(p, n):
        e = pair_ref[p]
        mine = (e >> 24) & 1
        order_two = (e >> 25) & 1
        courier_two = mine * two_ref[(e >> 9) & 31]
        e = e & 0xFFFFFF
        list_ref[n] = e
        n = n + mine
        list_ref[n] = e + 257
        n = n + courier_two
        list_ref[n] = e + 65536
        n = n + order_two
        list_ref[n] = e + 65536 + 257
        return n + (order_two & courier_two)

    n = lax.fori_loop(0, OB_DEV * ADJ, one_pair, jnp.int32(0), unroll=8)
    for i in range(REST):
        list_ref[n + i] = jnp.int32(NO_ORDER * 65536 + NO_COURIER * 256)
    rounds_ref[0] = (n + REST - 1) // REST


def first_list_kernel(pair_ref, early_ref, late_ref, early_rounds_ref, late_rounds_ref, has_ref):
    def one_block(b, counts):
        early_n, late_n = counts
        early_any, late_any = jnp.int32(0), jnp.int32(0)
        for i in range(ADJ):
            e = pair_ref[b * ADJ + i]
            early = (e >> 24) & 1
            late = (e >> 25) & 1
            two = (e >> 26) & 1
            e = e & 0xFFFFFF
            early_any, late_any = early_any | early, late_any | late
            for step, more in ((0, 1), (257, 1), (65536, two), (65536 + 257, two)):
                early_ref[early_n] = e + step
                late_ref[late_n] = e + step
                early_n = early_n + (early & more)
                late_n = late_n + (late & more)
        has_ref[b] = early_any
        has_ref[OB_DEV + b] = late_any
        return early_n, late_n

    counts = lax.fori_loop(0, OB_DEV, one_block, (jnp.int32(0), jnp.int32(0)))
    for n, list_ref, rounds_ref in ((counts[0], early_ref, early_rounds_ref), (counts[1], late_ref, late_rounds_ref)):
        for i in range(REST):
            list_ref[n + i] = jnp.int32(NO_ORDER * 65536 + NO_COURIER * 256)
        rounds_ref[0] = (n + REST - 1) // REST


def call_on_scalars(kernel, sizes, name, *operands):
    smem = pl.BlockSpec(memory_space=pltpu.SMEM)
    return pl.pallas_call(
        kernel,
        out_shape=tuple(jax.ShapeDtypeStruct((size,), jnp.int32) for size in sizes),
        in_specs=[smem] * len(operands),
        out_specs=(smem,) * len(sizes),
        compiler_params=pltpu.CompilerParams(vmem_limit_bytes=1024 * 1024),
        name=name,
    )(*operands)


def pair_fields(adjacency, order_count):
    flat = adjacency.reshape(-1)
    z = flat >> 2
    mine = jnp.where((flat & 3) == lax.axis_index("sub"), 1, 0)
    two = jnp.repeat(jnp.where(order_count > HALF, 1, 0), ADJ)
    block = jnp.arange(OB_DEV * ADJ, dtype=jnp.int32) // ADJ
    slot = slot_of(z, lax.axis_index("zone"))
    return (2 * block << 16) + (2 * z << 8), slot, mine, two


def first_lists(adjacency, order_count):
    entry, slot, mine, two = pair_fields(adjacency, order_count)
    is_early, place = early_slot(slot)
    entry = entry + 2 * jnp.where(is_early == 1, place, slot)
    pairs = entry + ((mine & is_early) << 24) + ((mine & (1 - is_early)) << 25) + (two << 26)
    sizes = (LIST_SIZE, LIST_SIZE, 1, 1, 2 * OB_DEV)
    return call_on_scalars(first_list_kernel, sizes, "first_lists", pairs.astype(jnp.int32))


def work_list(adjacency, order_count, courier_two):
    entry, slot, mine, two = pair_fields(adjacency, order_count)
    pairs = entry + 2 * slot + (mine << 24) + ((mine * two) << 25)
    return call_on_scalars(list_kernel, (LIST_SIZE, 1), "work_list", pairs.astype(jnp.int32), courier_two)


def pass_kernel(sum_couriers, list_ref, rounds_ref, summed_ref, kept_ref, weight_ref, live_ref, out_ref, w_ref, r_ref, m_ref):
    summed_blocks, kept_blocks = weight_ref.shape[0], live_ref.shape[0]
    rounds = rounds_ref[0]
    weight = weight_ref[...]

    high = weight.astype(jnp.bfloat16).astype(jnp.float32)
    low = weight - high
    blank = jnp.zeros((64 - 2 * summed_blocks, 128), jnp.float32)
    for part in range(2):
        rows = []
        for value in (high, low):
            rows += [value[:, part * 128 : part * 128 + 128], value[:, HALF + part * 128 : HALF + part * 128 + 128]]
            if summed_blocks < 32:
                rows.append(blank)
        w_ref[part * 128 : part * 128 + 128, :] = jnp.transpose(jnp.concatenate(rows, axis=0)).astype(jnp.bfloat16)
    r_ref[...] = jnp.zeros(r_ref.shape, jnp.float32)
    lanes = lax.broadcasted_iota(jnp.int32, (1, 128), 1) % 64

    def piece(e):
        order, courier, slot = e >> 16, (e >> 8) & 255, e & 255
        order_row = jnp.minimum(order, 2 * OB_DEV - 1) * HALF
        courier_row = (slot >> 1) * COURIER_ROWS + (slot & 1) * HALF
        return (courier, order, courier_row, order_row) if sum_couriers else (order, courier, order_row, courier_row)

    def sides(s_row, k_row):
        left = summed_ref[pl.ds(pl.multiple_of(s_row, 16), HALF), :]
        right = kept_ref[pl.ds(pl.multiple_of(k_row, 16), HALF), :]
        return left, right

    def scores(left, right):
        return lax.dot_general(left, right, (((1,), (1,)), ((), ())), preferred_element_type=jnp.float32)

    def weighted(s, s_row, k_row):
        left, right = sides(s_row, k_row)
        lane = (s % 2) * summed_blocks + s // 2
        ones = jnp.where(lanes == lane, 1.0, 0.0).astype(jnp.bfloat16)
        left = jnp.concatenate([left, w_ref[...]], axis=1)
        right = jnp.concatenate([right, jnp.broadcast_to(ones, (HALF, 128))], axis=1)
        return scores(left, right)

    def steps(first, count):
        todo = [piece(list_ref[first + t]) for t in range(count)]
        sums = [
            jnp.sum(jnp.exp2(weighted(s, s_row, k_row)).reshape(HALF // 8, 8, HALF), axis=0)
            for s, _, s_row, k_row in todo
        ]
        for (_, k, _, _), part in zip(todo, sums):
            r_ref[k // 2, k % 2] += part

    large_steps = rounds // (UNROLL // REST)

    def large_step(i, carry):
        steps(i * UNROLL, UNROLL)
        return carry

    def small_step(i, carry):
        steps(i * REST, REST)
        return carry

    lax.fori_loop(0, large_steps, large_step, 0)
    lax.fori_loop(large_steps * (UNROLL // REST), rounds, small_step, 0)

    large = jnp.where((weight > 0.5 * LOWEST) & ~(jnp.abs(weight) <= 128.0), 1.0, 0.0)
    bad = jnp.max(large, axis=0, keepdims=True)
    bad = jnp.maximum(bad[:, 0:HALF], bad[:, HALF:])
    for half in range(2):
        cut = slice(half * HALF, (half + 1) * HALF)
        total = jnp.sum(r_ref[0:kept_blocks, half], axis=1)
        live = live_ref[:, cut] > 0.5 * LOWEST
        fine = (total >= 2.0**-86) & (total <= 2.0**126)
        off = jnp.where(live & ~fine, 1.0, 0.0)
        bad = jnp.maximum(bad, jnp.max(off, axis=0, keepdims=True))
        out_ref[:, cut] = jnp.where(live, jnp.log2(jnp.where(live, total, 1.0)), LOWEST)
    bad = jnp.max(bad)

    @pl.when(bad > 0.0)
    def _():
        m_ref[...] = jnp.full(m_ref.shape, LOWEST, jnp.float32)
        r_ref[...] = jnp.zeros(r_ref.shape, jnp.float32)

        def one_piece(i, carry):
            s, k, s_row, k_row = piece(list_ref[i])
            block = jnp.minimum(s // 2, summed_blocks - 1)
            w = weight_ref[pl.ds(block, 1), pl.ds(pl.multiple_of((s % 2) * HALF, HALF), HALF)]
            column = jnp.transpose(jnp.broadcast_to(w, (128, HALF)))
            x = scores(*sides(s_row, k_row)) + jnp.concatenate([column, column], axis=1)
            before = m_ref[k // 2, k % 2, 0:1]
            after = jnp.maximum(before, jnp.max(x, axis=0, keepdims=True))
            scaled = r_ref[k // 2, k % 2, 0:1] * jnp.exp2(before - after)
            m_ref[k // 2, k % 2, 0:1] = after
            r_ref[k // 2, k % 2, 0:1] = scaled + jnp.sum(jnp.exp2(x - after), axis=0, keepdims=True)
            return carry

        lax.fori_loop(0, rounds * REST, one_piece, 0)
        for half in range(2):
            cut = slice(half * HALF, (half + 1) * HALF)
            live = live_ref[:, cut] > 0.5 * LOWEST
            total = jnp.where(live, r_ref[0:kept_blocks, half, 0, :], 1.0)
            out_ref[:, cut] = jnp.where(live, m_ref[0:kept_blocks, half, 0, :] + jnp.log2(total), LOWEST)


def half_sweep(sum_couriers, work, rounds, summed, kept, weight, live, name):
    smem = pl.BlockSpec(memory_space=pltpu.SMEM)
    vmem = pl.BlockSpec(memory_space=pltpu.VMEM)
    summed_blocks, kept_blocks = weight.shape[0], live.shape[0]

    def kernel(*refs):
        pass_kernel(sum_couriers, *refs)

    return pl.pallas_call(
        kernel,
        out_shape=jax.ShapeDtypeStruct((kept_blocks, BLOCK), jnp.float32),
        in_specs=[smem, smem] + [vmem] * 4,
        out_specs=vmem,
        scratch_shapes=pass_scratch(kept_blocks),
        compiler_params=pltpu.CompilerParams(vmem_limit_bytes=VMEM_LIMIT),
        cost_estimate=PASS_COST,
        name=name,
    )(work, rounds, summed, kept, weight, live)


PASS_COST = pl.CostEstimate(flops=28 * 2 * 512 * 512 * 128, bytes_accessed=6 << 20, transcendentals=28 * 512 * 512)


def pass_scratch(kept_blocks):
    return [
        pltpu.VMEM((HALF, 128), jnp.bfloat16),
        pltpu.VMEM((kept_blocks + 1, 2, 8, HALF), jnp.float32),
        pltpu.VMEM((kept_blocks + 1, 2, 8, HALF), jnp.float32),
    ]


def first_kernel(early, work_ref, rounds_ref, zone_ref, has_ref, *refs):
    count = len(EARLY) if early else PARTS
    parts, (orders_ref, live_ref, out_ref, couriers_ref, log_cap_ref, w_ref, r_ref, m_ref, weight_ref, here_ref, sem) = (
        refs[:count],
        refs[count:],
    )
    rows = couriers_ref.shape[0] // count
    copies = [
        pltpu.make_async_copy(part, couriers_ref.at[pl.ds(i * rows, rows), :], sem.at[i]) for i, part in enumerate(parts)
    ]
    for copy in copies:
        copy.start()
    for block in range(OB_DEV):
        named = has_ref[block if early else OB_DEV + block] > 0
        here_ref[block : block + 1, :] = jnp.where(named, live_ref[block : block + 1, :], LOWEST)
    for copy in copies:
        copy.wait()
    for zone in range(ZONES):
        slot = slot_of(jnp.int32(zone), zone_ref[0])
        if early:
            _, slot = early_slot(slot)
        row = slot * COURIER_ROWS + BLOCK
        tail = couriers_ref[pl.ds(pl.multiple_of(row, 16), 16), :].astype(jnp.float32)
        log_cap_ref[zone : zone + 1, :] = jnp.concatenate([tail[i : i + 1] for i in range(4)], axis=1)
    cap = log_cap_ref[...]
    live = cap > 0.0
    log_cap_ref[...] = jnp.where(live, jnp.log2(jnp.where(live, cap, 1.0)), LOWEST)
    weight_ref[...] = jnp.where(live, 0.0, LOWEST)
    pass_kernel(True, work_ref, rounds_ref, couriers_ref, orders_ref, weight_ref, here_ref, out_ref, w_ref, r_ref, m_ref)


def first_half_sweep(early, work, rounds, zone, has, parts, orders, live, name):
    smem = pl.BlockSpec(memory_space=pltpu.SMEM)
    vmem = pl.BlockSpec(memory_space=pltpu.VMEM)

    def kernel(*refs):
        first_kernel(early, *refs)

    couriers = (len(parts) * 4 * COURIER_ROWS, EMB)
    kept_out = () if early else (
        jax.ShapeDtypeStruct(couriers, jnp.bfloat16),
        jax.ShapeDtypeStruct((ZONES, BLOCK), jnp.float32),
    )
    as_scratch = [pltpu.VMEM(couriers, jnp.bfloat16), pltpu.VMEM((ZONES, BLOCK), jnp.float32)] if early else []
    return pl.pallas_call(
        kernel,
        out_shape=(jax.ShapeDtypeStruct((OB_DEV, BLOCK), jnp.float32),) + kept_out,
        in_specs=[smem] * 4 + [pl.BlockSpec(memory_space=pl.ANY)] * len(parts) + [vmem] * 2,
        out_specs=(vmem,) * (1 + len(kept_out)),
        scratch_shapes=as_scratch
        + pass_scratch(OB_DEV)
        + [
            pltpu.VMEM((ZONES, BLOCK), jnp.float32),
            pltpu.VMEM((OB_DEV, BLOCK), jnp.float32),
            pltpu.SemaphoreType.DMA((len(parts),)),
        ],
        compiler_params=pltpu.CompilerParams(vmem_limit_bytes=VMEM_LIMIT),
        cost_estimate=pl.CostEstimate(flops=14 * 2 * 512 * 512 * 128, bytes_accessed=6 << 20, transcendentals=14 * 512 * 512),
        name=name,
    )(work, rounds, zone.reshape(1), has, *parts, orders, live)


def shards(
    order_features,
    w_in,
    bias_in,
    w_out,
    bias_out,
    courier_embed,
    courier_cap,
    adjacency,
    order_count,
    courier_count,
):
    sub = lax.axis_index("sub")
    positions = jnp.arange(BLOCK, dtype=jnp.int32)

    own_live = positions < courier_count[0]
    row = gather_row(*pack(courier_count, courier_embed, courier_cap))
    lists = first_lists(adjacency, order_count)
    row, bias_in, lists = lax.optimization_barrier((row, bias_in, lists))
    early_list, late_list, early_rounds, late_rounds, has = lists
    orders = embed_orders(order_features, w_in, bias_in, w_out, bias_out)
    order_live = positions[None, :] < order_count[:, None]
    live = jnp.where(order_live, 0.0, LOWEST)
    zone = lax.axis_index("zone")

    own = [row] + [plane_step(row, 1, step) for step in (1, 2, 3)]
    other = [other_core(row)] + [None] * 3
    parts = own + other
    (early_partial,) = first_half_sweep(
        True, early_list, early_rounds, zone, has, [parts[p] for p in EARLY], orders, live, "orders_1_early"
    )
    own[1], own[2], own[3], early_partial = lax.optimization_barrier((own[1], own[2], own[3], early_partial))
    for step in (1, 2, 3):
        other[step] = other_core(own[step])
    late_partial, couriers, log_cap = first_half_sweep(
        False, late_list, late_rounds, zone, has, own + other, orders, live, "orders_1"
    )
    partial = join(early_partial, late_partial)

    mine = adjacency % SUBS == sub
    order_here = jnp.where(order_live & jnp.any(mine, axis=1, keepdims=True), 0.0, LOWEST)

    def order_dual_of(partial):
        return jnp.where(order_live, -join_subs(partial), LOWEST)

    courier_live = log_cap > 0.5 * LOWEST
    work, rounds = work_list(adjacency, order_count, courier_live[:, HALF].astype(jnp.int32))
    named = jnp.any(
        (adjacency.reshape(-1)[None, :] == jnp.arange(ZONES)[:, None] * SUBS + sub), axis=1, keepdims=True
    )
    courier_here = jnp.where(courier_live & named, 0.0, LOWEST)

    def courier_pass(order_dual, name):
        return half_sweep(False, work, rounds, orders, couriers, order_dual, courier_here, name)

    order_dual = order_dual_of(partial)
    sums = join_zones(courier_pass(order_dual, "couriers_1"))
    courier_dual = jnp.where(courier_live, log_cap - sums, LOWEST)
    order_dual = order_dual_of(half_sweep(True, work, rounds, couriers, orders, courier_dual, order_here, "orders_2"))
    partial = courier_pass(order_dual, "couriers_2")
    parts = lax.all_to_all(partial, "zone", 0, 0, tiled=True)
    highest = jnp.max(parts, axis=0)
    total = highest + jnp.log2(jnp.sum(jnp.exp2(parts - highest[None]), axis=0))
    own_log_cap = jnp.log2(courier_cap.astype(jnp.float32))
    courier_out = jnp.where(own_live, DUAL_SCALE * (own_log_cap - total), 0.0)
    order_out = jnp.where(order_live, DUAL_SCALE * order_dual, 0.0)
    return order_out.reshape(-1), courier_out


def solution(mesh):
    return jax.shard_map(
        shards,
        mesh=mesh,
        in_specs=(
            P("zone", None),
            P(),
            P(),
            P(),
            P(),
            P(("zone", "sub"), None),
            P(("zone", "sub")),
            P("zone", None),
            P("zone"),
            P(("zone", "sub")),
        ),
        out_specs=(P("zone"), P(("zone", "sub"))),
        check_vma=False,
    )
```

profile of v0, /device:TPU:1, one launch (start us, length us, event | category | flops | bytes accessed | tf_op | source)
XLA Modules:
  0.0 210.9 jit_solution(12621192981932455516)
XLA Ops:
  2.3 3.6 %collective-permute-start.2 = (bf16[528,128]{1,0:T(8,128)(2,1)S(1)}, bf16[528,128]{1,0:T(8,128)(2,1)S(1)}, u32[]{:S(2)}, u32[]{:S(2)}) collective-permute-start(bf16[528,128]{1,0:T(8,128)(2,1)S(1)} %get-tuple-element.26), channel_id=1, source_target_pairs={{0,24},{4,100},{8,0},{12,108},{16,8},{20,116},{24,16},{28,124},{32... | collective-permute-start | bytes 405512 | tf_op jit(solution)/shard_map/ppermute | solution.py:54
  8.7 2.7 %first_lists.1 = (s32[272]{0:T(512)S(1)}, s32[272]{0:T(512)S(1)}, s32[1]{0:T(128)}, s32[1]{0:T(128)}, s32[32]{0:T(128)S(1)}) custom-call(s32[128]{0:T(128)S(1)} %get-tuple-element.52.pair_ref), custom_call_target="tpu_custom_call" | custom-call | tf_op jit(solution)/shard_map/first_lists/pallas_call | solution.py:244
  11.3 1.7 collective-permute-done
  13.1 1.6 collective-permute-start.6
  17.3 6.6 %embed_orders.1.refs_6_.refs_12_.refs_2_.refs_3_ = bf16[8192,128]{1,0:T(8,128)(2,1)S(1)} custom-call(bf16[8192,128]{1,0:T(8,128)(2,1)} %x_hbm.1, bf16[128,512]{1,0:T(8,128)(2,1)} %w_in_hbm.1, f32[1,512]{1,0:T(1,128)} %bitcast.19, bf16[512,128]{1,0:T(8,128)(2,1)} %w_out_hbm.1, f32[1,128]{1,0:T(1,128)} %bitcast.20), custom_call_target="tpu_custom_call" | custom-call | flops 2147483648 | bytes 4194304 | tf_op jit(solution)/shard_map/embed_orders/pallas_call | solution.py:178
  24.0 9.8 %orders_1_early.1 = f32[16,512]{1,0:T(8,128)S(1)} custom-call(s32[272]{0:T(512)S(1)} %get-tuple-element.36.refs_0_, s32[1]{0:T(128)} %get-tuple-element.37.refs_1_, s32[1]{0:T(128)} %bitcast.refs_2_, s32[32]{0:T(128)S(1)} %get-tuple-element.34.refs_3_, bf16[2112,128]{1,0:T(8,128)(2,1)S(1)} %constant_dynamic-update-slice_fusion.refs_4_, ...), custom_call_target="tpu_custom_call" | custom-call | flops 939524096 | bytes 6291456 | tf_op jit(solution)/shard_map/orders_1_early/pallas_call | solution.py:455
  33.8 4.9 %collective-permute-start.7 = (bf16[2112,128]{1,0:T(8,128)(2,1)S(1)}, bf16[2112,128]{1,0:T(8,128)(2,1)S(1)}, u32[]{:S(2)}, u32[]{:S(2)}) collective-permute-start(bf16[2112,128]{1,0:T(8,128)(2,1)S(1)} %collective-permute-done.3.refs_5_), channel_id=1, source_target_pairs={{0,4},{4,0},{8,12},{12,8},{16,20},{20,16},{24,28},{28,24},{32,36},... | collective-permute-start | bytes 1622024 | tf_op jit(solution)/shard_map/ppermute | solution.py:42
  41.8 24.3 %orders_1.1 = (f32[16,512]{1,0:T(8,128)S(1)}, bf16[16896,128]{1,0:T(8,128)(2,1)S(1)}, f32[32,512]{1,0:T(8,128)S(1)}) custom-call(s32[272]{0:T(512)S(1)} %get-tuple-element.32.refs_0_, s32[1]{0:T(128)} %get-tuple-element.33.refs_1_, s32[1]{0:T(128)} %bitcast.refs_2_, s32[32]{0:T(128)S(1)} %get-tuple-element.34.refs_3_, ...), custom_call_target="tpu_custom_call" | custom-call | flops 939524096 | bytes 6291456 | tf_op jit(solution)/shard_map/orders_1/pallas_call | solution.py:455
  66.2 3.9 %collective-permute-start.11 = (f32[16,512]{1,0:T(8,128)S(1)}, f32[16,512]{1,0:T(8,128)S(1)}, u32[]{:S(2)}, u32[]{:S(2)}) collective-permute-start(f32[16,512]{1,0:T(8,128)S(1)} %multiply_add_fusion.2), channel_id=1, source_target_pairs={{0,2},{1,3},{2,0},{3,1},{4,6},{5,7},{6,4},{7,5},{8,10},{9,11},{10,... | collective-permute-start | bytes 98312 | tf_op jit(solution)/shard_map/ppermute | solution.py:46
  70.8 2.2 %work_list.1 = (s32[272]{0:T(512)S(1)}, s32[1]{0:T(128)}) custom-call(s32[128]{0:T(128)S(1)} %shift-left_add_fusion.1.pair_ref, s32[32]{0:T(128)S(1)} %convert_reduce_fusion.two_ref), custom_call_target="tpu_custom_call" | custom-call | tf_op jit(solution)/shard_map/work_list/pallas_call | solution.py:244
  74.1 23.8 %couriers_1.1 = f32[32,512]{1,0:T(8,128)S(1)} custom-call(s32[272]{0:T(512)S(1)} %get-tuple-element.43.refs_0_, s32[1]{0:T(128)} %get-tuple-element.44.refs_1_, bf16[8192,128]{1,0:T(8,128)(2,1)S(1)} %embed_orders.1.refs_6_.refs_12_.refs_2_.refs_3_, bf16[16896,128]{1,0:T(8,128)(2,1)S(1)} %get-tuple-element.45.refs_3_.refs_2_, ...), custom_call_target="tpu_custom_call" | custom-call | flops 1879048192 | bytes 6291456 | tf_op jit(solution)/shard_map/couriers_1/pallas_call | solution.py:388
  98.0 7.0 %collective-permute-start.13 = (f32[32,512]{1,0:T(8,128)S(1)}, f32[32,512]{1,0:T(8,128)S(1)}, u32[]{:S(2)}, u32[]{:S(2)}) collective-permute-start(f32[32,512]{1,0:T(8,128)S(1)} %couriers_1.1), channel_id=1, source_target_pairs={{0,4},{4,0},{8,12},{12,8},{16,20},{20,16},{24,28},{28,24},{32,36},... | collective-permute-start | bytes 196616 | tf_op jit(solution)/shard_map/ppermute | solution.py:42
  106.0 7.2 %collective-permute-start.16 = (f32[32,512]{1,0:T(8,128)S(1)}, f32[32,512]{1,0:T(8,128)S(1)}, u32[]{:S(2)}, u32[]{:S(2)}) collective-permute-start(f32[32,512]{1,0:T(8,128)S(1)} %multiply_add_fusion.1), channel_id=1, source_target_pairs={{0,24},{4,100},{8,0},{12,108},{16,8},{20,116},{24,16},{28,124},{32... | collective-permute-start | bytes 196616 | tf_op jit(solution)/shard_map/ppermute | solution.py:54
  113.2 1.9 collective-permute-start.15
  115.2 2.6 %collective-permute-done.15 = f32[32,512]{1,0:T(8,128)S(1)} collective-permute-done((f32[32,512]{1,0:T(8,128)S(1)}, f32[32,512]{1,0:T(8,128)S(1)}, u32[]{:S(2)}, u32[]{:S(2)}) %collective-permute-start.15) | collective-permute-done | bytes 65568 | tf_op jit(solution)/shard_map/ppermute | solution.py:54
  117.8 1.6 collective-permute-done.14
  119.5 3.0 %collective-permute-start.18 = (f32[32,512]{1,0:T(8,128)S(1)}, f32[32,512]{1,0:T(8,128)S(1)}, u32[]{:S(2)}, u32[]{:S(2)}) collective-permute-start(f32[32,512]{1,0:T(8,128)S(1)} %multiply_add_fusion), channel_id=1, source_target_pairs={{0,64},{4,20},{8,72},{12,28},{16,80},{20,4},{24,88},{28,12},{32,96... | collective-permute-start | bytes 196616 | tf_op jit(solution)/shard_map/ppermute | solution.py:54
  124.2 2.6 %collective-permute-done.17 = f32[32,512]{1,0:T(8,128)S(1)} collective-permute-done((f32[32,512]{1,0:T(8,128)S(1)}, f32[32,512]{1,0:T(8,128)S(1)}, u32[]{:S(2)}, u32[]{:S(2)}) %collective-permute-start.17) | collective-permute-done | bytes 65568 | tf_op jit(solution)/shard_map/ppermute | solution.py:54
  127.0 23.6 %orders_2.1 = f32[16,512]{1,0:T(8,128)S(1)} custom-call(s32[272]{0:T(512)S(1)} %get-tuple-element.43.refs_0_, s32[1]{0:T(128)} %get-tuple-element.44.refs_1_, bf16[16896,128]{1,0:T(8,128)(2,1)S(1)} %get-tuple-element.45.refs_3_.refs_2_, bf16[8192,128]{1,0:T(8,128)(2,1)S(1)} %embed_orders.1.refs_6_.refs_12_.refs_2_.refs_3_, ...), custom_call_target="tpu_custom_call" | custom-call | flops 1879048192 | bytes 6291456 | tf_op jit(solution)/shard_map/orders_2/pallas_call | solution.py:388
  150.7 1.4 collective-permute-start.20
  153.4 1.6 collective-permute-done.21
  155.9 23.8 %couriers_2.1 = f32[32,512]{1,0:T(8,128)S(1)} custom-call(s32[272]{0:T(512)S(1)} %get-tuple-element.43.refs_0_, s32[1]{0:T(128)} %get-tuple-element.44.refs_1_, bf16[8192,128]{1,0:T(8,128)(2,1)S(1)} %embed_orders.1.refs_6_.refs_12_.refs_2_.refs_3_, bf16[16896,128]{1,0:T(8,128)(2,1)S(1)} %get-tuple-element.45.refs_3_.refs_2_, ...), custom_call_target="tpu_custom_call" | custom-call | flops 1879048192 | bytes 6291456 | tf_op jit(solution)/shard_map/couriers_2/pallas_call | solution.py:388
  180.4 22.5 %all-to-all-start = ((f32[32,1,512]{2,1,0:T(1,128)}), f32[32,1,512]{2,1,0:T(1,128)S(1)}, u32[]{:S(2)}, u32[]{:S(2)}) async-start(f32[32,1,512]{2,1,0:T(1,128)} %copy.17), calls=%async_computation | async-start | bytes 131072 | tf_op jit(solution)/shard_map/all_to_all | solution.py:533
  203.5 6.7 %all-to-all-done = f32[32,1,512]{2,1,0:T(1,128)S(1)} async-done(((f32[32,1,512]{2,1,0:T(1,128)}), f32[32,1,512]{2,1,0:T(1,128)S(1)}, u32[]{:S(2)}, u32[]{:S(2)}) %all-to-all-start) | async-done | bytes 65568 | tf_op jit(solution)/shard_map/all_to_all | solution.py:533
  (66 shorter events, 18.8 us)
Async XLA Ops:
  2.3 10.8 %collective-permute-start.2 = (bf16[528,128]{1,0:T(8,128)(2,1)S(1)}, bf16[528,128]{1,0:T(8,128)(2,1)S(1)}, u32[]{:S(2)}, u32[]{:S(2)}) collective-permute-start(bf16[528,128]{1,0:T(8,128)(2,1)S(1)} %get-tuple-element.26), channel_id=1, source_target_pairs={{0,24},{4,100},{8,0},{12,108},{16,8},{20,116},{24,16},{28,124},{32... | collective-permute-start | bytes 405512 | tf_op jit(solution)/shard_map/ppermute | solution.py:54
  5.9 7.1 %collective-permute-start.1 = (bf16[528,128]{1,0:T(8,128)(2,1)S(1)}, bf16[528,128]{1,0:T(8,128)(2,1)S(1)}, u32[]{:S(2)}, u32[]{:S(2)}) collective-permute-start(bf16[528,128]{1,0:T(8,128)(2,1)S(1)} %get-tuple-element.26), channel_id=1, source_target_pairs={{0,16},{4,68},{8,24},{12,76},{16,0},{20,84},{24,8},{28,92},{32,48}... | collective-permute-start | bytes 405512 | tf_op jit(solution)/shard_map/ppermute | solution.py:54
  6.3 6.8 %collective-permute-start = (bf16[528,128]{1,0:T(8,128)(2,1)S(1)}, bf16[528,128]{1,0:T(8,128)(2,1)S(1)}, u32[]{:S(2)}, u32[]{:S(2)}) collective-permute-start(bf16[528,128]{1,0:T(8,128)(2,1)S(1)} %get-tuple-element.26), channel_id=1, source_target_pairs={{0,8},{4,36},{8,16},{12,44},{16,24},{20,52},{24,0},{28,60},{32,40}... | collective-permute-start | bytes 405512 | tf_op jit(solution)/shard_map/ppermute | solution.py:54
  13.1 10.8 %collective-permute-start.6 = (bf16[2112,128]{1,0:T(8,128)(2,1)S(1)}, bf16[2112,128]{1,0:T(8,128)(2,1)S(1)}, u32[]{:S(2)}, u32[]{:S(2)}) collective-permute-start(bf16[2112,128]{1,0:T(8,128)(2,1)S(1)} %constant_dynamic-update-slice_fusion.refs_4_), channel_id=1, source_target_pairs={{0,4},{4,0},{8,12},{12,8},{16,20},{20,16},{24,28},{28,24},{32,36},... | collective-permute-start | bytes 1622024 | tf_op jit(solution)/shard_map/ppermute | solution.py:42
  14.8 19.0 %collective-permute-start.5 = (bf16[2112,128]{1,0:T(8,128)(2,1)S(1)}, bf16[2112,128]{1,0:T(8,128)(2,1)S(1)}, u32[]{:S(2)}, u32[]{:S(2)}) collective-permute-start(bf16[2112,128]{1,0:T(8,128)(2,1)S(1)} %constant_dynamic-update-slice_fusion.refs_4_), channel_id=1, source_target_pairs={{0,96},{4,28},{8,104},{12,4},{16,112},{20,12},{24,120},{28,20},{32... | collective-permute-start | bytes 1622024 | tf_op jit(solution)/shard_map/ppermute | solution.py:54
  15.5 18.3 %collective-permute-start.4 = (bf16[2112,128]{1,0:T(8,128)(2,1)S(1)}, bf16[2112,128]{1,0:T(8,128)(2,1)S(1)}, u32[]{:S(2)}, u32[]{:S(2)}) collective-permute-start(bf16[2112,128]{1,0:T(8,128)(2,1)S(1)} %constant_dynamic-update-slice_fusion.refs_4_), channel_id=1, source_target_pairs={{0,64},{4,20},{8,72},{12,28},{16,80},{20,4},{24,88},{28,12},{32,96... | collective-permute-start | bytes 1622024 | tf_op jit(solution)/shard_map/ppermute | solution.py:54
  16.2 17.6 %collective-permute-start.3 = (bf16[2112,128]{1,0:T(8,128)(2,1)S(1)}, bf16[2112,128]{1,0:T(8,128)(2,1)S(1)}, u32[]{:S(2)}, u32[]{:S(2)}) collective-permute-start(bf16[2112,128]{1,0:T(8,128)(2,1)S(1)} %constant_dynamic-update-slice_fusion.refs_4_), channel_id=1, source_target_pairs={{0,32},{4,12},{8,40},{12,20},{16,48},{20,28},{24,56},{28,4},{32,64... | collective-permute-start | bytes 1622024 | tf_op jit(solution)/shard_map/ppermute | solution.py:54
  33.8 6.4 %collective-permute-start.7 = (bf16[2112,128]{1,0:T(8,128)(2,1)S(1)}, bf16[2112,128]{1,0:T(8,128)(2,1)S(1)}, u32[]{:S(2)}, u32[]{:S(2)}) collective-permute-start(bf16[2112,128]{1,0:T(8,128)(2,1)S(1)} %collective-permute-done.3.refs_5_), channel_id=1, source_target_pairs={{0,4},{4,0},{8,12},{12,8},{16,20},{20,16},{24,28},{28,24},{32,36},... | collective-permute-start | bytes 1622024 | tf_op jit(solution)/shard_map/ppermute | solution.py:42
  38.7 2.3 %collective-permute-start.8 = (bf16[2112,128]{1,0:T(8,128)(2,1)S(1)}, bf16[2112,128]{1,0:T(8,128)(2,1)S(1)}, u32[]{:S(2)}, u32[]{:S(2)}) collective-permute-start(bf16[2112,128]{1,0:T(8,128)(2,1)S(1)} %collective-permute-done.4.refs_6_), channel_id=1, source_target_pairs={{0,4},{4,0},{8,12},{12,8},{16,20},{20,16},{24,28},{28,24},{32,36},... | collective-permute-start | bytes 1622024 | tf_op jit(solution)/shard_map/ppermute | solution.py:42
  38.8 3.0 %collective-permute-start.9 = (bf16[2112,128]{1,0:T(8,128)(2,1)S(1)}, bf16[2112,128]{1,0:T(8,128)(2,1)S(1)}, u32[]{:S(2)}, u32[]{:S(2)}) collective-permute-start(bf16[2112,128]{1,0:T(8,128)(2,1)S(1)} %collective-permute-done.5.refs_7_), channel_id=1, source_target_pairs={{0,4},{4,0},{8,12},{12,8},{16,20},{20,16},{24,28},{28,24},{32,36},... | collective-permute-start | bytes 1622024 | tf_op jit(solution)/shard_map/ppermute | solution.py:42
  66.1 6.9 %collective-permute-start.12 = (f32[16,512]{1,0:T(8,128)S(1)}, f32[16,512]{1,0:T(8,128)S(1)}, u32[]{:S(2)}, u32[]{:S(2)}) collective-permute-start(f32[16,512]{1,0:T(8,128)S(1)} %multiply_add_fusion.2), channel_id=1, source_target_pairs={{0,3},{1,0},{2,1},{3,2},{4,7},{5,4},{6,5},{7,6},{8,11},{9,8},{10,9... | collective-permute-start | bytes 98312 | tf_op jit(solution)/shard_map/ppermute | solution.py:46
  66.2 6.8 %collective-permute-start.11 = (f32[16,512]{1,0:T(8,128)S(1)}, f32[16,512]{1,0:T(8,128)S(1)}, u32[]{:S(2)}, u32[]{:S(2)}) collective-permute-start(f32[16,512]{1,0:T(8,128)S(1)} %multiply_add_fusion.2), channel_id=1, source_target_pairs={{0,2},{1,3},{2,0},{3,1},{4,6},{5,7},{6,4},{7,5},{8,10},{9,11},{10,... | collective-permute-start | bytes 98312 | tf_op jit(solution)/shard_map/ppermute | solution.py:46
  70.1 4.0 %collective-permute-start.10 = (f32[16,512]{1,0:T(8,128)S(1)}, f32[16,512]{1,0:T(8,128)S(1)}, u32[]{:S(2)}, u32[]{:S(2)}) collective-permute-start(f32[16,512]{1,0:T(8,128)S(1)} %multiply_add_fusion.2), channel_id=1, source_target_pairs={{0,1},{1,2},{2,3},{3,0},{4,5},{5,6},{6,7},{7,4},{8,9},{9,10},{10,1... | collective-permute-start | bytes 98312 | tf_op jit(solution)/shard_map/ppermute | solution.py:46
  98.0 8.0 %collective-permute-start.13 = (f32[32,512]{1,0:T(8,128)S(1)}, f32[32,512]{1,0:T(8,128)S(1)}, u32[]{:S(2)}, u32[]{:S(2)}) collective-permute-start(f32[32,512]{1,0:T(8,128)S(1)} %couriers_1.1), channel_id=1, source_target_pairs={{0,4},{4,0},{8,12},{12,8},{16,20},{20,16},{24,28},{28,24},{32,36},... | collective-permute-start | bytes 196616 | tf_op jit(solution)/shard_map/ppermute | solution.py:42
  106.0 9.3 %collective-permute-start.16 = (f32[32,512]{1,0:T(8,128)S(1)}, f32[32,512]{1,0:T(8,128)S(1)}, u32[]{:S(2)}, u32[]{:S(2)}) collective-permute-start(f32[32,512]{1,0:T(8,128)S(1)} %multiply_add_fusion.1), channel_id=1, source_target_pairs={{0,24},{4,100},{8,0},{12,108},{16,8},{20,116},{24,16},{28,124},{32... | collective-permute-start | bytes 196616 | tf_op jit(solution)/shard_map/ppermute | solution.py:54
  113.2 4.6 %collective-permute-start.15 = (f32[32,512]{1,0:T(8,128)S(1)}, f32[32,512]{1,0:T(8,128)S(1)}, u32[]{:S(2)}, u32[]{:S(2)}) collective-permute-start(f32[32,512]{1,0:T(8,128)S(1)} %multiply_add_fusion.1), channel_id=1, source_target_pairs={{0,16},{4,68},{8,24},{12,76},{16,0},{20,84},{24,8},{28,92},{32,48}... | collective-permute-start | bytes 196616 | tf_op jit(solution)/shard_map/ppermute | solution.py:54
  115.1 4.3 %collective-permute-start.14 = (f32[32,512]{1,0:T(8,128)S(1)}, f32[32,512]{1,0:T(8,128)S(1)}, u32[]{:S(2)}, u32[]{:S(2)}) collective-permute-start(f32[32,512]{1,0:T(8,128)S(1)} %multiply_add_fusion.1), channel_id=1, source_target_pairs={{0,8},{4,36},{8,16},{12,44},{16,24},{20,52},{24,0},{28,60},{32,40}... | collective-permute-start | bytes 196616 | tf_op jit(solution)/shard_map/ppermute | solution.py:54
  119.5 3.9 %collective-permute-start.19 = (f32[32,512]{1,0:T(8,128)S(1)}, f32[32,512]{1,0:T(8,128)S(1)}, u32[]{:S(2)}, u32[]{:S(2)}) collective-permute-start(f32[32,512]{1,0:T(8,128)S(1)} %multiply_add_fusion), channel_id=1, source_target_pairs={{0,96},{4,28},{8,104},{12,4},{16,112},{20,12},{24,120},{28,20},{32... | collective-permute-start | bytes 196616 | tf_op jit(solution)/shard_map/ppermute | solution.py:54
  119.5 4.7 %collective-permute-start.18 = (f32[32,512]{1,0:T(8,128)S(1)}, f32[32,512]{1,0:T(8,128)S(1)}, u32[]{:S(2)}, u32[]{:S(2)}) collective-permute-start(f32[32,512]{1,0:T(8,128)S(1)} %multiply_add_fusion), channel_id=1, source_target_pairs={{0,64},{4,20},{8,72},{12,28},{16,80},{20,4},{24,88},{28,12},{32,96... | collective-permute-start | bytes 196616 | tf_op jit(solution)/shard_map/ppermute | solution.py:54
  122.5 4.3 %collective-permute-start.17 = (f32[32,512]{1,0:T(8,128)S(1)}, f32[32,512]{1,0:T(8,128)S(1)}, u32[]{:S(2)}, u32[]{:S(2)}) collective-permute-start(f32[32,512]{1,0:T(8,128)S(1)} %multiply_add_fusion), channel_id=1, source_target_pairs={{0,32},{4,12},{8,40},{12,20},{16,48},{20,28},{24,56},{28,4},{32,64... | collective-permute-start | bytes 196616 | tf_op jit(solution)/shard_map/ppermute | solution.py:54
  150.6 2.8 %collective-permute-start.22 = (f32[16,512]{1,0:T(8,128)S(1)}, f32[16,512]{1,0:T(8,128)S(1)}, u32[]{:S(2)}, u32[]{:S(2)}) collective-permute-start(f32[16,512]{1,0:T(8,128)S(1)} %orders_2.1), channel_id=1, source_target_pairs={{0,3},{1,0},{2,1},{3,2},{4,7},{5,4},{6,5},{7,6},{8,11},{9,8},{10,9... | collective-permute-start | bytes 98312 | tf_op jit(solution)/shard_map/ppermute | solution.py:46
  150.7 4.3 %collective-permute-start.21 = (f32[16,512]{1,0:T(8,128)S(1)}, f32[16,512]{1,0:T(8,128)S(1)}, u32[]{:S(2)}, u32[]{:S(2)}) collective-permute-start(f32[16,512]{1,0:T(8,128)S(1)} %orders_2.1), channel_id=1, source_target_pairs={{0,2},{1,3},{2,0},{3,1},{4,6},{5,7},{6,4},{7,5},{8,10},{9,11},{10,... | collective-permute-start | bytes 98312 | tf_op jit(solution)/shard_map/ppermute | solution.py:46
  150.7 5.1 %collective-permute-start.20 = (f32[16,512]{1,0:T(8,128)S(1)}, f32[16,512]{1,0:T(8,128)S(1)}, u32[]{:S(2)}, u32[]{:S(2)}) collective-permute-start(f32[16,512]{1,0:T(8,128)S(1)} %orders_2.1), channel_id=1, source_target_pairs={{0,1},{1,2},{2,3},{3,0},{4,5},{5,6},{6,7},{7,4},{8,9},{9,10},{10,1... | collective-permute-start | bytes 98312 | tf_op jit(solution)/shard_map/ppermute | solution.py:46
  180.4 29.8 %all-to-all-start = ((f32[32,1,512]{2,1,0:T(1,128)}), f32[32,1,512]{2,1,0:T(1,128)S(1)}, u32[]{:S(2)}, u32[]{:S(2)}) async-start(f32[32,1,512]{2,1,0:T(1,128)} %copy.17), calls=%async_computation | async-start | bytes 131072 | tf_op jit(solution)/shard_map/all_to_all | solution.py:533
  (3 other events, 104.3 us)
where the time goes:
time: 211 us
  Pallas kernels  118 us (56%)
  starting transfers between devices  62.1 us (29%)
  waiting for transfers between devices  24.3 us (12%)
  other arithmetic  2.9 us (1%)
  local copies, waits for them, and re-layouts  2.4 us (1%)
    pallas_call x3, Pallas kernels, half_sweep(): pl.pallas_call(kernel, out_shape=jax.ShapeDtypeStruct((kept_blocks, BLOCK...  71.3 us
    pallas_call x2, Pallas kernels, first_half_sweep(): pl.pallas_call(kernel, out_shape=(jax.ShapeDtypeStruct((OB_DEV, BLOCK), j...  34.1 us
    all_to_all x1, starting transfers between devices, shards(): parts = lax.all_to_all(partial, 'zone', 0, 0, tiled=True)  22.5 us
    ppermute x12, starting transfers between devices, plane_step(): return lax.ppermute(value, 'zone', pairs)  19.5 us
    ppermute x5, starting transfers between devices, other_core(): lax.ppermute(value, 'zone', [(zone_of(y, x, c), zone_of(y, x, 1 - c)) for...  14.1 us
    ppermute x12, waiting for transfers between devices, plane_step(): return lax.ppermute(value, 'zone', pairs)  9.6 us
    all_to_all x1, waiting for transfers between devices, shards(): parts = lax.all_to_all(partial, 'zone', 0, 0, tiled=True)  6.7 us
    pallas_call x1, Pallas kernels, embed_orders(): pl.pallas_call(embed_kernel, out_shape=jax.ShapeDtypeStruct((rows, EMB),...  6.62 us
  transfers between devices with their start and end apart: 24, of which 15 were waited for; matrix products, arithmetic and copies ran while one was open for 2% of the time, Pallas kernels for 10%

commit v1 on v0

--- a/solution.py
+++ b/solution.py
@@ -412,7 +412,7 @@
     count = len(EARLY) if early else PARTS
     parts, (orders_ref, live_ref, out_ref, couriers_ref, log_cap_ref, w_ref, r_ref, m_ref, weight_ref, here_ref, sem) = (
         refs[:count],
-        refs[count:],
+        refs[-11:],
     )
     rows = couriers_ref.shape[0] // count
     copies = [
@@ -446,7 +446,7 @@
     def kernel(*refs):
         first_kernel(early, *refs)
 
-    couriers = (len(parts) * 4 * COURIER_ROWS, EMB)
+    couriers = ((len(EARLY) if early else PARTS) * 4 * COURIER_ROWS, EMB)
     kept_out = () if early else (
         jax.ShapeDtypeStruct(couriers, jnp.bfloat16),
         jax.ShapeDtypeStruct((ZONES, BLOCK), jnp.float32),
@@ -497,13 +497,15 @@
 
     own = [row] + [plane_step(row, 1, step) for step in (1, 2, 3)]
     other = [other_core(row)] + [None] * 3
+    for step in (3, 2):
+        own[step], orders = lax.optimization_barrier((own[step], orders))
+        other[step] = other_core(own[step])
     parts = own + other
     (early_partial,) = first_half_sweep(
-        True, early_list, early_rounds, zone, has, [parts[p] for p in EARLY], orders, live, "orders_1_early"
+        True, early_list, early_rounds, zone, has, [parts[p] for p in (*EARLY, 2, 3)], orders, live, "orders_1_early"
     )
-    own[1], own[2], own[3], early_partial = lax.optimization_barrier((own[1], own[2], own[3], early_partial))
-    for step in (1, 2, 3):
-        other[step] = other_core(own[step])
+    own[1], early_partial = lax.optimization_barrier((own[1], early_partial))
+    other[1] = other_core(own[1])
     late_partial, couriers, log_cap = first_half_sweep(
         False, late_list, late_rounds, zone, has, own + other, orders, live, "orders_1"
     )

time: 211 us -> 227 us (1.076)
  Pallas kernels: 118 us -> 138 us
  starting transfers between devices: 62.1 us -> 56.6 us
    pallas_call x3, Pallas kernels: 71.3 us -> 86.7 us  [half_sweep(): pl.pallas_call(kernel, out_shape=jax.ShapeDtypeStruct((kept_blocks, BLOCK...]
    ppermute x5, starting transfers between devices: 14.1 us -> 7.14 us  [other_core(): lax.ppermute(value, 'zone', [(zone_of(y, x, c), zone_of(y, x, 1 - c)) for...]
    ppermute x12, starting transfers between devices: 19.5 us -> 25.1 us  [plane_step(): return lax.ppermute(value, 'zone', pairs)]
    all_to_all x1, starting transfers between devices: 22.5 us -> 17.4 us  [shards(): parts = lax.all_to_all(partial, 'zone', 0, 0, tiled=True)]
    pallas_call x2, Pallas kernels: 34.1 us -> 38.6 us  [first_half_sweep(): pl.pallas_call(kernel, out_shape=(jax.ShapeDtypeStruct((OB_DEV, BLOCK), j...]
    ppermute x12, waiting for transfers between devices: 9.6 us -> 12.1 us  [plane_step(): return lax.ppermute(value, 'zone', pairs)]
  transfers between devices with their start and end apart: 24 -> 24, of which waited for: 15 -> 14; matrix products, arithmetic and copies ran while one was open for 2% -> 2% of each run, Pallas kernels for 10% -> 10%
where the time goes in v1:
time: 227 us
  Pallas kernels  138 us (61%)
  starting transfers between devices  56.6 us (25%)
  waiting for transfers between devices  25.9 us (11%)
  other arithmetic  2.9 us (1%)
  local copies, waits for them, and re-layouts  2.4 us (1%)
    pallas_call x3, Pallas kernels, half_sweep(): pl.pallas_call(kernel, out_shape=jax.ShapeDtypeStruct((kept_blocks, BLOCK...  86.7 us
    pallas_call x2, Pallas kernels, first_half_sweep(): pl.pallas_call(kernel, out_shape=(jax.ShapeDtypeStruct((OB_DEV, BLOCK), j...  38.6 us
    ppermute x12, starting transfers between devices, plane_step(): return lax.ppermute(value, 'zone', pairs)  25.1 us
    all_to_all x1, starting transfers between devices, shards(): parts = lax.all_to_all(partial, 'zone', 0, 0, tiled=True)  17.4 us
    ppermute x12, waiting for transfers between devices, plane_step(): return lax.ppermute(value, 'zone', pairs)  12.1 us
    ppermute x5, starting transfers between devices, other_core(): lax.ppermute(value, 'zone', [(zone_of(y, x, c), zone_of(y, x, 1 - c)) for...  7.14 us
    ppermute x6, starting transfers between devices, along_z(): lax.ppermute(value, 'sub', [(i, (i + step) % SUBS) for i in range(SUBS)])  6.87 us
    all_to_all x1, waiting for transfers between devices, shards(): parts = lax.all_to_all(partial, 'zone', 0, 0, tiled=True)  6.7 us
  transfers between devices with their start and end apart: 24, of which 14 were waited for; matrix products, arithmetic and copies ran while one was open for 2% of the time, Pallas kernels for 10%

profile of v1, /device:TPU:1, one launch (start us, length us, event | category | flops | bytes accessed | tf_op | source)
XLA Modules:
  0.0 227.1 jit_solution(7716625182326339322)
XLA Ops:
  2.3 3.6 %collective-permute-start.2 = (bf16[528,128]{1,0:T(8,128)(2,1)S(1)}, bf16[528,128]{1,0:T(8,128)(2,1)S(1)}, u32[]{:S(2)}, u32[]{:S(2)}) collective-permute-start(bf16[528,128]{1,0:T(8,128)(2,1)S(1)} %get-tuple-element.28), channel_id=1, source_target_pairs={{0,24},{4,100},{8,0},{12,108},{16,8},{20,116},{24,16},{28,124},{32... | collective-permute-start | bytes 405512 | tf_op jit(solution)/shard_map/ppermute | solution.py:54
  8.7 2.7 %first_lists.1 = (s32[272]{0:T(512)S(1)}, s32[272]{0:T(512)S(1)}, s32[1]{0:T(128)}, s32[1]{0:T(128)}, s32[32]{0:T(128)S(1)}) custom-call(s32[128]{0:T(128)S(1)} %get-tuple-element.56.pair_ref), custom_call_target="tpu_custom_call" | custom-call | tf_op jit(solution)/shard_map/first_lists/pallas_call | solution.py:244
  11.3 1.7 collective-permute-done
  13.1 2.3 collective-permute-start.6
  15.9 2.5 %collective-permute-start.4 = (bf16[2112,128]{1,0:T(8,128)(2,1)S(1)}, bf16[2112,128]{1,0:T(8,128)(2,1)S(1)}, u32[]{:S(2)}, u32[]{:S(2)}) collective-permute-start(bf16[2112,128]{1,0:T(8,128)(2,1)S(1)} %constant_dynamic-update-slice_fusion.refs_4_), channel_id=1, source_target_pairs={{0,4},{4,0},{8,12},{12,8},{16,20},{20,16},{24,28},{28,24},{32,36},... | collective-permute-start | bytes 1622024 | tf_op jit(solution)/shard_map/ppermute | solution.py:42
  19.1 6.6 %embed_orders.1.refs_8_.refs_12_.refs_2_.refs_3_ = bf16[8192,128]{1,0:T(8,128)(2,1)S(1)} custom-call(bf16[8192,128]{1,0:T(8,128)(2,1)} %x_hbm.1, bf16[128,512]{1,0:T(8,128)(2,1)} %w_in_hbm.1, f32[1,512]{1,0:T(1,128)} %bitcast.19, bf16[512,128]{1,0:T(8,128)(2,1)} %w_out_hbm.1, f32[1,128]{1,0:T(1,128)} %bitcast.20), custom_call_target="tpu_custom_call" | custom-call | flops 2147483648 | bytes 4194304 | tf_op jit(solution)/shard_map/embed_orders/pallas_call | solution.py:178
  25.8 1.7 collective-permute-done.6.refs_7_
  27.5 3.0 %collective-permute-start.8 = (bf16[2112,128]{1,0:T(8,128)(2,1)S(1)}, bf16[2112,128]{1,0:T(8,128)(2,1)S(1)}, u32[]{:S(2)}, u32[]{:S(2)}) collective-permute-start(bf16[2112,128]{1,0:T(8,128)(2,1)S(1)} %collective-permute-done.5.refs_6_), channel_id=1, source_target_pairs={{0,4},{4,0},{8,12},{12,8},{16,20},{20,16},{24,28},{28,24},{32,36},... | collective-permute-start | bytes 1622024 | tf_op jit(solution)/shard_map/ppermute | solution.py:42
  30.5 11.7 %orders_1_early.1 = f32[16,512]{1,0:T(8,128)S(1)} custom-call(s32[272]{0:T(512)S(1)} %get-tuple-element.38.refs_0_, s32[1]{0:T(128)} %get-tuple-element.39.refs_1_, s32[1]{0:T(128)} %bitcast.refs_2_, s32[32]{0:T(128)S(1)} %get-tuple-element.36.refs_3_, bf16[2112,128]{1,0:T(8,128)(2,1)S(1)} %constant_dynamic-update-slice_fusion.refs_4_, ...), custom_call_target="tpu_custom_call" | custom-call | flops 939524096 | bytes 6291456 | tf_op jit(solution)/shard_map/orders_1_early/pallas_call | solution.py:455
  44.4 26.9 %orders_1.1 = (f32[16,512]{1,0:T(8,128)S(1)}, bf16[16896,128]{1,0:T(8,128)(2,1)S(1)}, f32[32,512]{1,0:T(8,128)S(1)}) custom-call(s32[272]{0:T(512)S(1)} %get-tuple-element.34.refs_0_, s32[1]{0:T(128)} %get-tuple-element.35.refs_1_, s32[1]{0:T(128)} %bitcast.refs_2_, s32[32]{0:T(128)S(1)} %get-tuple-element.36.refs_3_, ...), custom_call_target="tpu_custom_call" | custom-call | flops 939524096 | bytes 6291456 | tf_op jit(solution)/shard_map/orders_1/pallas_call | solution.py:455
  71.3 4.5 %collective-permute-start.12 = (f32[16,512]{1,0:T(8,128)S(1)}, f32[16,512]{1,0:T(8,128)S(1)}, u32[]{:S(2)}, u32[]{:S(2)}) collective-permute-start(f32[16,512]{1,0:T(8,128)S(1)} %multiply_add_fusion.2), channel_id=1, source_target_pairs={{0,3},{1,0},{2,1},{3,2},{4,7},{5,4},{6,5},{7,6},{8,11},{9,8},{10,9... | collective-permute-start | bytes 98312 | tf_op jit(solution)/shard_map/ppermute | solution.py:46
  76.8 2.2 work_list.1
  80.2 29.0 %couriers_1.1 = f32[32,512]{1,0:T(8,128)S(1)} custom-call(s32[272]{0:T(512)S(1)} %get-tuple-element.47.refs_0_, s32[1]{0:T(128)} %get-tuple-element.48.refs_1_, bf16[8192,128]{1,0:T(8,128)(2,1)S(1)} %embed_orders.1.refs_8_.refs_12_.refs_2_.refs_3_, bf16[16896,128]{1,0:T(8,128)(2,1)S(1)} %get-tuple-element.49.refs_3_.refs_2_, ...), custom_call_target="tpu_custom_call" | custom-call | flops 1879048192 | bytes 6291456 | tf_op jit(solution)/shard_map/couriers_1/pallas_call | solution.py:388
  111.3 3.5 %collective-permute-start.16 = (f32[32,512]{1,0:T(8,128)S(1)}, f32[32,512]{1,0:T(8,128)S(1)}, u32[]{:S(2)}, u32[]{:S(2)}) collective-permute-start(f32[32,512]{1,0:T(8,128)S(1)} %multiply_add_fusion.1), channel_id=1, source_target_pairs={{0,24},{4,100},{8,0},{12,108},{16,8},{20,116},{24,16},{28,124},{32... | collective-permute-start | bytes 196616 | tf_op jit(solution)/shard_map/ppermute | solution.py:54
  114.7 4.4 %collective-permute-start.15 = (f32[32,512]{1,0:T(8,128)S(1)}, f32[32,512]{1,0:T(8,128)S(1)}, u32[]{:S(2)}, u32[]{:S(2)}) collective-permute-start(f32[32,512]{1,0:T(8,128)S(1)} %multiply_add_fusion.1), channel_id=1, source_target_pairs={{0,16},{4,68},{8,24},{12,76},{16,0},{20,84},{24,8},{28,92},{32,48}... | collective-permute-start | bytes 196616 | tf_op jit(solution)/shard_map/ppermute | solution.py:54
  119.1 1.6 collective-permute-done.15
  120.8 2.7 %collective-permute-done.14 = f32[32,512]{1,0:T(8,128)S(1)} collective-permute-done((f32[32,512]{1,0:T(8,128)S(1)}, f32[32,512]{1,0:T(8,128)S(1)}, u32[]{:S(2)}, u32[]{:S(2)}) %collective-permute-start.14) | collective-permute-done | bytes 65568 | tf_op jit(solution)/shard_map/ppermute | solution.py:54
  123.5 9.2 %collective-permute-start.19 = (f32[32,512]{1,0:T(8,128)S(1)}, f32[32,512]{1,0:T(8,128)S(1)}, u32[]{:S(2)}, u32[]{:S(2)}) collective-permute-start(f32[32,512]{1,0:T(8,128)S(1)} %multiply_add_fusion), channel_id=1, source_target_pairs={{0,96},{4,28},{8,104},{12,4},{16,112},{20,12},{24,120},{28,20},{32... | collective-permute-start | bytes 196616 | tf_op jit(solution)/shard_map/ppermute | solution.py:54
  134.6 2.8 %collective-permute-done.18 = f32[32,512]{1,0:T(8,128)S(1)} collective-permute-done((f32[32,512]{1,0:T(8,128)S(1)}, f32[32,512]{1,0:T(8,128)S(1)}, u32[]{:S(2)}, u32[]{:S(2)}) %collective-permute-start.18) | collective-permute-done | bytes 65568 | tf_op jit(solution)/shard_map/ppermute | solution.py:54
  137.8 28.8 %orders_2.1 = f32[16,512]{1,0:T(8,128)S(1)} custom-call(s32[272]{0:T(512)S(1)} %get-tuple-element.47.refs_0_, s32[1]{0:T(128)} %get-tuple-element.48.refs_1_, bf16[16896,128]{1,0:T(8,128)(2,1)S(1)} %get-tuple-element.49.refs_3_.refs_2_, bf16[8192,128]{1,0:T(8,128)(2,1)S(1)} %embed_orders.1.refs_8_.refs_12_.refs_2_.refs_3_, ...), custom_call_target="tpu_custom_call" | custom-call | flops 1879048192 | bytes 6291456 | tf_op jit(solution)/shard_map/orders_2/pallas_call | solution.py:388
  169.4 1.6 collective-permute-done.21
  171.9 29.0 %couriers_2.1 = f32[32,512]{1,0:T(8,128)S(1)} custom-call(s32[272]{0:T(512)S(1)} %get-tuple-element.47.refs_0_, s32[1]{0:T(128)} %get-tuple-element.48.refs_1_, bf16[8192,128]{1,0:T(8,128)(2,1)S(1)} %embed_orders.1.refs_8_.refs_12_.refs_2_.refs_3_, bf16[16896,128]{1,0:T(8,128)(2,1)S(1)} %get-tuple-element.49.refs_3_.refs_2_, ...), custom_call_target="tpu_custom_call" | custom-call | flops 1879048192 | bytes 6291456 | tf_op jit(solution)/shard_map/couriers_2/pallas_call | solution.py:388
  201.6 17.4 %all-to-all-start = ((f32[32,1,512]{2,1,0:T(1,128)}), f32[32,1,512]{2,1,0:T(1,128)S(1)}, u32[]{:S(2)}, u32[]{:S(2)}) async-start(f32[32,1,512]{2,1,0:T(1,128)} %copy.17), calls=%async_computation | async-start | bytes 131072 | tf_op jit(solution)/shard_map/all_to_all | solution.py:535
  219.7 6.7 %all-to-all-done = f32[32,1,512]{2,1,0:T(1,128)S(1)} async-done(((f32[32,1,512]{2,1,0:T(1,128)}), f32[32,1,512]{2,1,0:T(1,128)S(1)}, u32[]{:S(2)}, u32[]{:S(2)}) %all-to-all-start) | async-done | bytes 65568 | tf_op jit(solution)/shard_map/all_to_all | solution.py:535
  (66 shorter events, 19.6 us)
Async XLA Ops:
  2.3 10.8 %collective-permute-start.2 = (bf16[528,128]{1,0:T(8,128)(2,1)S(1)}, bf16[528,128]{1,0:T(8,128)(2,1)S(1)}, u32[]{:S(2)}, u32[]{:S(2)}) collective-permute-start(bf16[528,128]{1,0:T(8,128)(2,1)S(1)} %get-tuple-element.28), channel_id=1, source_target_pairs={{0,24},{4,100},{8,0},{12,108},{16,8},{20,116},{24,16},{28,124},{32... | collective-permute-start | bytes 405512 | tf_op jit(solution)/shard_map/ppermute | solution.py:54
  5.9 7.1 %collective-permute-start.1 = (bf16[528,128]{1,0:T(8,128)(2,1)S(1)}, bf16[528,128]{1,0:T(8,128)(2,1)S(1)}, u32[]{:S(2)}, u32[]{:S(2)}) collective-permute-start(bf16[528,128]{1,0:T(8,128)(2,1)S(1)} %get-tuple-element.28), channel_id=1, source_target_pairs={{0,16},{4,68},{8,24},{12,76},{16,0},{20,84},{24,8},{28,92},{32,48}... | collective-permute-start | bytes 405512 | tf_op jit(solution)/shard_map/ppermute | solution.py:54
  6.3 6.8 %collective-permute-start = (bf16[528,128]{1,0:T(8,128)(2,1)S(1)}, bf16[528,128]{1,0:T(8,128)(2,1)S(1)}, u32[]{:S(2)}, u32[]{:S(2)}) collective-permute-start(bf16[528,128]{1,0:T(8,128)(2,1)S(1)} %get-tuple-element.28), channel_id=1, source_target_pairs={{0,8},{4,36},{8,16},{12,44},{16,24},{20,52},{24,0},{28,60},{32,40}... | collective-permute-start | bytes 405512 | tf_op jit(solution)/shard_map/ppermute | solution.py:54
  13.1 14.3 %collective-permute-start.6 = (bf16[2112,128]{1,0:T(8,128)(2,1)S(1)}, bf16[2112,128]{1,0:T(8,128)(2,1)S(1)}, u32[]{:S(2)}, u32[]{:S(2)}) collective-permute-start(bf16[2112,128]{1,0:T(8,128)(2,1)S(1)} %constant_dynamic-update-slice_fusion.refs_4_), channel_id=1, source_target_pairs={{0,96},{4,28},{8,104},{12,4},{16,112},{20,12},{24,120},{28,20},{32... | collective-permute-start | bytes 1622024 | tf_op jit(solution)/shard_map/ppermute | solution.py:54
  15.4 12.1 %collective-permute-start.5 = (bf16[2112,128]{1,0:T(8,128)(2,1)S(1)}, bf16[2112,128]{1,0:T(8,128)(2,1)S(1)}, u32[]{:S(2)}, u32[]{:S(2)}) collective-permute-start(bf16[2112,128]{1,0:T(8,128)(2,1)S(1)} %constant_dynamic-update-slice_fusion.refs_4_), channel_id=1, source_target_pairs={{0,64},{4,20},{8,72},{12,28},{16,80},{20,4},{24,88},{28,12},{32,96... | collective-permute-start | bytes 1622024 | tf_op jit(solution)/shard_map/ppermute | solution.py:54
  15.9 14.5 %collective-permute-start.4 = (bf16[2112,128]{1,0:T(8,128)(2,1)S(1)}, bf16[2112,128]{1,0:T(8,128)(2,1)S(1)}, u32[]{:S(2)}, u32[]{:S(2)}) collective-permute-start(bf16[2112,128]{1,0:T(8,128)(2,1)S(1)} %constant_dynamic-update-slice_fusion.refs_4_), channel_id=1, source_target_pairs={{0,4},{4,0},{8,12},{12,8},{16,20},{20,16},{24,28},{28,24},{32,36},... | collective-permute-start | bytes 1622024 | tf_op jit(solution)/shard_map/ppermute | solution.py:42
  18.4 23.8 %collective-permute-start.3 = (bf16[2112,128]{1,0:T(8,128)(2,1)S(1)}, bf16[2112,128]{1,0:T(8,128)(2,1)S(1)}, u32[]{:S(2)}, u32[]{:S(2)}) collective-permute-start(bf16[2112,128]{1,0:T(8,128)(2,1)S(1)} %constant_dynamic-update-slice_fusion.refs_4_), channel_id=1, source_target_pairs={{0,32},{4,12},{8,40},{12,20},{16,48},{20,28},{24,56},{28,4},{32,64... | collective-permute-start | bytes 1622024 | tf_op jit(solution)/shard_map/ppermute | solution.py:54
  27.5 16.9 %collective-permute-start.8 = (bf16[2112,128]{1,0:T(8,128)(2,1)S(1)}, bf16[2112,128]{1,0:T(8,128)(2,1)S(1)}, u32[]{:S(2)}, u32[]{:S(2)}) collective-permute-start(bf16[2112,128]{1,0:T(8,128)(2,1)S(1)} %collective-permute-done.5.refs_6_), channel_id=1, source_target_pairs={{0,4},{4,0},{8,12},{12,8},{16,20},{20,16},{24,28},{28,24},{32,36},... | collective-permute-start | bytes 1622024 | tf_op jit(solution)/shard_map/ppermute | solution.py:42
  30.4 13.9 %collective-permute-start.9 = (bf16[2112,128]{1,0:T(8,128)(2,1)S(1)}, bf16[2112,128]{1,0:T(8,128)(2,1)S(1)}, u32[]{:S(2)}, u32[]{:S(2)}) collective-permute-start(bf16[2112,128]{1,0:T(8,128)(2,1)S(1)} %collective-permute-done.6.refs_7_), channel_id=1, source_target_pairs={{0,4},{4,0},{8,12},{12,8},{16,20},{20,16},{24,28},{28,24},{32,36},... | collective-permute-start | bytes 1622024 | tf_op jit(solution)/shard_map/ppermute | solution.py:42
  42.2 2.1 collective-permute-start.7
  71.3 7.7 %collective-permute-start.12 = (f32[16,512]{1,0:T(8,128)S(1)}, f32[16,512]{1,0:T(8,128)S(1)}, u32[]{:S(2)}, u32[]{:S(2)}) collective-permute-start(f32[16,512]{1,0:T(8,128)S(1)} %multiply_add_fusion.2), channel_id=1, source_target_pairs={{0,3},{1,0},{2,1},{3,2},{4,7},{5,4},{6,5},{7,6},{8,11},{9,8},{10,9... | collective-permute-start | bytes 98312 | tf_op jit(solution)/shard_map/ppermute | solution.py:46
  75.8 4.4 %collective-permute-start.11 = (f32[16,512]{1,0:T(8,128)S(1)}, f32[16,512]{1,0:T(8,128)S(1)}, u32[]{:S(2)}, u32[]{:S(2)}) collective-permute-start(f32[16,512]{1,0:T(8,128)S(1)} %multiply_add_fusion.2), channel_id=1, source_target_pairs={{0,2},{1,3},{2,0},{3,1},{4,6},{5,7},{6,4},{7,5},{8,10},{9,11},{10,... | collective-permute-start | bytes 98312 | tf_op jit(solution)/shard_map/ppermute | solution.py:46
  75.8 4.4 %collective-permute-start.10 = (f32[16,512]{1,0:T(8,128)S(1)}, f32[16,512]{1,0:T(8,128)S(1)}, u32[]{:S(2)}, u32[]{:S(2)}) collective-permute-start(f32[16,512]{1,0:T(8,128)S(1)} %multiply_add_fusion.2), channel_id=1, source_target_pairs={{0,1},{1,2},{2,3},{3,0},{4,5},{5,6},{6,7},{7,4},{8,9},{9,10},{10,1... | collective-permute-start | bytes 98312 | tf_op jit(solution)/shard_map/ppermute | solution.py:46
  109.2 2.0 collective-permute-start.13
  111.3 7.9 %collective-permute-start.16 = (f32[32,512]{1,0:T(8,128)S(1)}, f32[32,512]{1,0:T(8,128)S(1)}, u32[]{:S(2)}, u32[]{:S(2)}) collective-permute-start(f32[32,512]{1,0:T(8,128)S(1)} %multiply_add_fusion.1), channel_id=1, source_target_pairs={{0,24},{4,100},{8,0},{12,108},{16,8},{20,116},{24,16},{28,124},{32... | collective-permute-start | bytes 196616 | tf_op jit(solution)/shard_map/ppermute | solution.py:54
  114.7 6.0 %collective-permute-start.15 = (f32[32,512]{1,0:T(8,128)S(1)}, f32[32,512]{1,0:T(8,128)S(1)}, u32[]{:S(2)}, u32[]{:S(2)}) collective-permute-start(f32[32,512]{1,0:T(8,128)S(1)} %multiply_add_fusion.1), channel_id=1, source_target_pairs={{0,16},{4,68},{8,24},{12,76},{16,0},{20,84},{24,8},{28,92},{32,48}... | collective-permute-start | bytes 196616 | tf_op jit(solution)/shard_map/ppermute | solution.py:54
  119.1 4.3 %collective-permute-start.14 = (f32[32,512]{1,0:T(8,128)S(1)}, f32[32,512]{1,0:T(8,128)S(1)}, u32[]{:S(2)}, u32[]{:S(2)}) collective-permute-start(f32[32,512]{1,0:T(8,128)S(1)} %multiply_add_fusion.1), channel_id=1, source_target_pairs={{0,8},{4,36},{8,16},{12,44},{16,24},{20,52},{24,0},{28,60},{32,40}... | collective-permute-start | bytes 196616 | tf_op jit(solution)/shard_map/ppermute | solution.py:54
  123.5 11.1 %collective-permute-start.19 = (f32[32,512]{1,0:T(8,128)S(1)}, f32[32,512]{1,0:T(8,128)S(1)}, u32[]{:S(2)}, u32[]{:S(2)}) collective-permute-start(f32[32,512]{1,0:T(8,128)S(1)} %multiply_add_fusion), channel_id=1, source_target_pairs={{0,96},{4,28},{8,104},{12,4},{16,112},{20,12},{24,120},{28,20},{32... | collective-permute-start | bytes 196616 | tf_op jit(solution)/shard_map/ppermute | solution.py:54
  132.7 4.7 %collective-permute-start.18 = (f32[32,512]{1,0:T(8,128)S(1)}, f32[32,512]{1,0:T(8,128)S(1)}, u32[]{:S(2)}, u32[]{:S(2)}) collective-permute-start(f32[32,512]{1,0:T(8,128)S(1)} %multiply_add_fusion), channel_id=1, source_target_pairs={{0,64},{4,20},{8,72},{12,28},{16,80},{20,4},{24,88},{28,12},{32,96... | collective-permute-start | bytes 196616 | tf_op jit(solution)/shard_map/ppermute | solution.py:54
  132.7 5.0 %collective-permute-start.17 = (f32[32,512]{1,0:T(8,128)S(1)}, f32[32,512]{1,0:T(8,128)S(1)}, u32[]{:S(2)}, u32[]{:S(2)}) collective-permute-start(f32[32,512]{1,0:T(8,128)S(1)} %multiply_add_fusion), channel_id=1, source_target_pairs={{0,32},{4,12},{8,40},{12,20},{16,48},{20,28},{24,56},{28,4},{32,64... | collective-permute-start | bytes 196616 | tf_op jit(solution)/shard_map/ppermute | solution.py:54
  166.6 2.8 %collective-permute-start.22 = (f32[16,512]{1,0:T(8,128)S(1)}, f32[16,512]{1,0:T(8,128)S(1)}, u32[]{:S(2)}, u32[]{:S(2)}) collective-permute-start(f32[16,512]{1,0:T(8,128)S(1)} %orders_2.1), channel_id=1, source_target_pairs={{0,3},{1,0},{2,1},{3,2},{4,7},{5,4},{6,5},{7,6},{8,11},{9,8},{10,9... | collective-permute-start | bytes 98312 | tf_op jit(solution)/shard_map/ppermute | solution.py:46
  166.7 4.3 %collective-permute-start.21 = (f32[16,512]{1,0:T(8,128)S(1)}, f32[16,512]{1,0:T(8,128)S(1)}, u32[]{:S(2)}, u32[]{:S(2)}) collective-permute-start(f32[16,512]{1,0:T(8,128)S(1)} %orders_2.1), channel_id=1, source_target_pairs={{0,2},{1,3},{2,0},{3,1},{4,6},{5,7},{6,4},{7,5},{8,10},{9,11},{10,... | collective-permute-start | bytes 98312 | tf_op jit(solution)/shard_map/ppermute | solution.py:46
  166.8 5.1 %collective-permute-start.20 = (f32[16,512]{1,0:T(8,128)S(1)}, f32[16,512]{1,0:T(8,128)S(1)}, u32[]{:S(2)}, u32[]{:S(2)}) collective-permute-start(f32[16,512]{1,0:T(8,128)S(1)} %orders_2.1), channel_id=1, source_target_pairs={{0,1},{1,2},{2,3},{3,0},{4,5},{5,6},{6,7},{7,4},{8,9},{9,10},{10,1... | collective-permute-start | bytes 98312 | tf_op jit(solution)/shard_map/ppermute | solution.py:46
  201.6 24.8 %all-to-all-start = ((f32[32,1,512]{2,1,0:T(1,128)}), f32[32,1,512]{2,1,0:T(1,128)S(1)}, u32[]{:S(2)}, u32[]{:S(2)}) async-start(f32[32,1,512]{2,1,0:T(1,128)} %copy.17), calls=%async_computation | async-start | bytes 131072 | tf_op jit(solution)/shard_map/all_to_all | solution.py:535
  (3 other events, 104.1 us)

commit v2 on v0

--- a/solution.py
+++ b/solution.py
@@ -130,7 +130,7 @@
 
 def join_zones(value):
     value = join(value, other_core(value))
-    for stage in range(2):
+    for stage in (1, 0):
         value = join(value, *[plane_step(value, stage, step) for step in (1, 2, 3)])
     return value
 

time: 211 us -> 225 us (1.066)
  Pallas kernels: 118 us -> 128 us
  starting transfers between devices: 62.1 us -> 67.2 us
    ppermute x12, starting transfers between devices: 19.5 us -> 10.8 us  [plane_step(): return lax.ppermute(value, 'zone', pairs)]
    pallas_call x3, Pallas kernels: 71.3 us -> 79 us  [half_sweep(): pl.pallas_call(kernel, out_shape=jax.ShapeDtypeStruct((kept_blocks, BLOCK...]
    ppermute x5, starting transfers between devices: 14.1 us -> 19.4 us  [other_core(): lax.ppermute(value, 'zone', [(zone_of(y, x, c), zone_of(y, x, 1 - c)) for...]
    ppermute x6, starting transfers between devices: 6.04 us -> 10.3 us  [along_z(): lax.ppermute(value, 'sub', [(i, (i + step) % SUBS) for i in range(SUBS)])]
    all_to_all x1, starting transfers between devices: 22.5 us -> 26.7 us  [shards(): parts = lax.all_to_all(partial, 'zone', 0, 0, tiled=True)]
    pallas_call x2, Pallas kernels: 34.1 us -> 36.7 us  [first_half_sweep(): pl.pallas_call(kernel, out_shape=(jax.ShapeDtypeStruct((OB_DEV, BLOCK), j...]
  transfers between devices with their start and end apart: 24 -> 24, of which waited for: 15 -> 15; matrix products, arithmetic and copies ran while one was open for 2% -> 2% of each run, Pallas kernels for 10% -> 9%
where the time goes in v2:
time: 225 us; the launch traced here: 226 us
  Pallas kernels  128 us (57%)
  starting transfers between devices  67.2 us (30%)
  waiting for transfers between devices  24 us (11%)
  other arithmetic  2.9 us (1%)
  local copies, waits for them, and re-layouts  2.4 us (1%)
    pallas_call x3, Pallas kernels, half_sweep(): pl.pallas_call(kernel, out_shape=jax.ShapeDtypeStruct((kept_blocks, BLOCK...  79 us
    pallas_call x2, Pallas kernels, first_half_sweep(): pl.pallas_call(kernel, out_shape=(jax.ShapeDtypeStruct((OB_DEV, BLOCK), j...  36.7 us
    all_to_all x1, starting transfers between devices, shards(): parts = lax.all_to_all(partial, 'zone', 0, 0, tiled=True)  26.7 us
    ppermute x5, starting transfers between devices, other_core(): lax.ppermute(value, 'zone', [(zone_of(y, x, c), zone_of(y, x, 1 - c)) for...  19.4 us
    ppermute x12, starting transfers between devices, plane_step(): return lax.ppermute(value, 'zone', pairs)  10.8 us
    ppermute x6, starting transfers between devices, along_z(): lax.ppermute(value, 'sub', [(i, (i + step) % SUBS) for i in range(SUBS)])  10.3 us
    ppermute x12, waiting for transfers between devices, plane_step(): return lax.ppermute(value, 'zone', pairs)  9.61 us
    all_to_all x1, waiting for transfers between devices, shards(): parts = lax.all_to_all(partial, 'zone', 0, 0, tiled=True)  6.81 us
  transfers between devices with their start and end apart: 24, of which 15 were waited for; matrix products, arithmetic and copies ran while one was open for 2% of the time, Pallas kernels for 9%

profile of v2, /device:TPU:1, one launch (start us, length us, event | category | flops | bytes accessed | tf_op | source)
XLA Modules:
  0.0 226.1 jit_solution(4644242644973690169)
XLA Ops:
  2.3 3.6 %collective-permute-start.2 = (bf16[528,128]{1,0:T(8,128)(2,1)S(1)}, bf16[528,128]{1,0:T(8,128)(2,1)S(1)}, u32[]{:S(2)}, u32[]{:S(2)}) collective-permute-start(bf16[528,128]{1,0:T(8,128)(2,1)S(1)} %get-tuple-element.26), channel_id=1, source_target_pairs={{0,24},{4,100},{8,0},{12,108},{16,8},{20,116},{24,16},{28,124},{32... | collective-permute-start | bytes 405512 | tf_op jit(solution)/shard_map/ppermute | solution.py:54
  8.7 2.7 %first_lists.1 = (s32[272]{0:T(512)S(1)}, s32[272]{0:T(512)S(1)}, s32[1]{0:T(128)}, s32[1]{0:T(128)}, s32[32]{0:T(128)S(1)}) custom-call(s32[128]{0:T(128)S(1)} %get-tuple-element.52.pair_ref), custom_call_target="tpu_custom_call" | custom-call | tf_op jit(solution)/shard_map/first_lists/pallas_call | solution.py:244
  11.3 1.7 collective-permute-done
  13.1 1.6 collective-permute-start.6
  17.3 6.6 %embed_orders.1.refs_6_.refs_12_.refs_2_.refs_3_ = bf16[8192,128]{1,0:T(8,128)(2,1)S(1)} custom-call(bf16[8192,128]{1,0:T(8,128)(2,1)} %x_hbm.1, bf16[128,512]{1,0:T(8,128)(2,1)} %w_in_hbm.1, f32[1,512]{1,0:T(1,128)} %bitcast.19, bf16[512,128]{1,0:T(8,128)(2,1)} %w_out_hbm.1, f32[1,128]{1,0:T(1,128)} %bitcast.20), custom_call_target="tpu_custom_call" | custom-call | flops 2147483648 | bytes 4194304 | tf_op jit(solution)/shard_map/embed_orders/pallas_call | solution.py:178
  24.0 9.8 %orders_1_early.1 = f32[16,512]{1,0:T(8,128)S(1)} custom-call(s32[272]{0:T(512)S(1)} %get-tuple-element.36.refs_0_, s32[1]{0:T(128)} %get-tuple-element.37.refs_1_, s32[1]{0:T(128)} %bitcast.refs_2_, s32[32]{0:T(128)S(1)} %get-tuple-element.34.refs_3_, bf16[2112,128]{1,0:T(8,128)(2,1)S(1)} %constant_dynamic-update-slice_fusion.refs_4_, ...), custom_call_target="tpu_custom_call" | custom-call | flops 939524096 | bytes 6291456 | tf_op jit(solution)/shard_map/orders_1_early/pallas_call | solution.py:455
  33.8 4.9 %collective-permute-start.7 = (bf16[2112,128]{1,0:T(8,128)(2,1)S(1)}, bf16[2112,128]{1,0:T(8,128)(2,1)S(1)}, u32[]{:S(2)}, u32[]{:S(2)}) collective-permute-start(bf16[2112,128]{1,0:T(8,128)(2,1)S(1)} %collective-permute-done.3.refs_5_), channel_id=1, source_target_pairs={{0,4},{4,0},{8,12},{12,8},{16,20},{20,16},{24,28},{28,24},{32,36},... | collective-permute-start | bytes 1622024 | tf_op jit(solution)/shard_map/ppermute | solution.py:42
  41.8 26.9 %orders_1.1 = (f32[16,512]{1,0:T(8,128)S(1)}, bf16[16896,128]{1,0:T(8,128)(2,1)S(1)}, f32[32,512]{1,0:T(8,128)S(1)}) custom-call(s32[272]{0:T(512)S(1)} %get-tuple-element.32.refs_0_, s32[1]{0:T(128)} %get-tuple-element.33.refs_1_, s32[1]{0:T(128)} %bitcast.refs_2_, s32[32]{0:T(128)S(1)} %get-tuple-element.34.refs_3_, ...), custom_call_target="tpu_custom_call" | custom-call | flops 939524096 | bytes 6291456 | tf_op jit(solution)/shard_map/orders_1/pallas_call | solution.py:455
  68.7 4.5 %collective-permute-start.12 = (f32[16,512]{1,0:T(8,128)S(1)}, f32[16,512]{1,0:T(8,128)S(1)}, u32[]{:S(2)}, u32[]{:S(2)}) collective-permute-start(f32[16,512]{1,0:T(8,128)S(1)} %multiply_add_fusion.2), channel_id=1, source_target_pairs={{0,3},{1,0},{2,1},{3,2},{4,7},{5,4},{6,5},{7,6},{8,11},{9,8},{10,9... | collective-permute-start | bytes 98312 | tf_op jit(solution)/shard_map/ppermute | solution.py:46
  74.2 2.2 work_list.1
  77.6 26.4 %couriers_1.1 = f32[32,512]{1,0:T(8,128)S(1)} custom-call(s32[272]{0:T(512)S(1)} %get-tuple-element.43.refs_0_, s32[1]{0:T(128)} %get-tuple-element.44.refs_1_, bf16[8192,128]{1,0:T(8,128)(2,1)S(1)} %embed_orders.1.refs_6_.refs_12_.refs_2_.refs_3_, bf16[16896,128]{1,0:T(8,128)(2,1)S(1)} %get-tuple-element.45.refs_3_.refs_2_, ...), custom_call_target="tpu_custom_call" | custom-call | flops 1879048192 | bytes 6291456 | tf_op jit(solution)/shard_map/couriers_1/pallas_call | solution.py:388
  104.0 12.4 %collective-permute-start.13 = (f32[32,512]{1,0:T(8,128)S(1)}, f32[32,512]{1,0:T(8,128)S(1)}, u32[]{:S(2)}, u32[]{:S(2)}) collective-permute-start(f32[32,512]{1,0:T(8,128)S(1)} %couriers_1.1), channel_id=1, source_target_pairs={{0,4},{4,0},{8,12},{12,8},{16,20},{20,16},{24,28},{28,24},{32,36},... | collective-permute-start | bytes 196616 | tf_op jit(solution)/shard_map/ppermute | solution.py:42
  117.6 1.4 collective-permute-start.14
  118.9 1.6 collective-permute-done.16
  120.6 1.6 collective-permute-done.15
  123.4 1.9 collective-permute-start.18
  126.5 1.6 collective-permute-done.18
  128.1 1.6 collective-permute-done.17
  129.8 26.2 %orders_2.1 = f32[16,512]{1,0:T(8,128)S(1)} custom-call(s32[272]{0:T(512)S(1)} %get-tuple-element.43.refs_0_, s32[1]{0:T(128)} %get-tuple-element.44.refs_1_, bf16[16896,128]{1,0:T(8,128)(2,1)S(1)} %get-tuple-element.45.refs_3_.refs_2_, bf16[8192,128]{1,0:T(8,128)(2,1)S(1)} %embed_orders.1.refs_6_.refs_12_.refs_2_.refs_3_, ...), custom_call_target="tpu_custom_call" | custom-call | flops 1879048192 | bytes 6291456 | tf_op jit(solution)/shard_map/orders_2/pallas_call | solution.py:388
  156.0 3.5 %collective-permute-start.22 = (f32[16,512]{1,0:T(8,128)S(1)}, f32[16,512]{1,0:T(8,128)S(1)}, u32[]{:S(2)}, u32[]{:S(2)}) collective-permute-start(f32[16,512]{1,0:T(8,128)S(1)} %orders_2.1), channel_id=1, source_target_pairs={{0,3},{1,0},{2,1},{3,2},{4,7},{5,4},{6,5},{7,6},{8,11},{9,8},{10,9... | collective-permute-start | bytes 98312 | tf_op jit(solution)/shard_map/ppermute | solution.py:46
  160.9 2.8 %collective-permute-done.21 = f32[16,512]{1,0:T(8,128)S(1)} collective-permute-done((f32[16,512]{1,0:T(8,128)S(1)}, f32[16,512]{1,0:T(8,128)S(1)}, u32[]{:S(2)}, u32[]{:S(2)}) %collective-permute-start.21) | collective-permute-done | bytes 32800 | tf_op jit(solution)/shard_map/ppermute | solution.py:46
  164.2 26.4 %couriers_2.1 = f32[32,512]{1,0:T(8,128)S(1)} custom-call(s32[272]{0:T(512)S(1)} %get-tuple-element.43.refs_0_, s32[1]{0:T(128)} %get-tuple-element.44.refs_1_, bf16[8192,128]{1,0:T(8,128)(2,1)S(1)} %embed_orders.1.refs_6_.refs_12_.refs_2_.refs_3_, bf16[16896,128]{1,0:T(8,128)(2,1)S(1)} %get-tuple-element.45.refs_3_.refs_2_, ...), custom_call_target="tpu_custom_call" | custom-call | flops 1879048192 | bytes 6291456 | tf_op jit(solution)/shard_map/couriers_2/pallas_call | solution.py:388
  191.3 26.7 %all-to-all-start = ((f32[32,1,512]{2,1,0:T(1,128)}), f32[32,1,512]{2,1,0:T(1,128)S(1)}, u32[]{:S(2)}, u32[]{:S(2)}) async-start(f32[32,1,512]{2,1,0:T(1,128)} %copy.17), calls=%async_computation | async-start | bytes 131072 | tf_op jit(solution)/shard_map/all_to_all | solution.py:533
  218.6 6.8 %all-to-all-done = f32[32,1,512]{2,1,0:T(1,128)S(1)} async-done(((f32[32,1,512]{2,1,0:T(1,128)}), f32[32,1,512]{2,1,0:T(1,128)S(1)}, u32[]{:S(2)}, u32[]{:S(2)}) %all-to-all-start) | async-done | bytes 65568 | tf_op jit(solution)/shard_map/all_to_all | solution.py:533
  (66 shorter events, 19.3 us)
Async XLA Ops:
  2.3 10.8 %collective-permute-start.2 = (bf16[528,128]{1,0:T(8,128)(2,1)S(1)}, bf16[528,128]{1,0:T(8,128)(2,1)S(1)}, u32[]{:S(2)}, u32[]{:S(2)}) collective-permute-start(bf16[528,128]{1,0:T(8,128)(2,1)S(1)} %get-tuple-element.26), channel_id=1, source_target_pairs={{0,24},{4,100},{8,0},{12,108},{16,8},{20,116},{24,16},{28,124},{32... | collective-permute-start | bytes 405512 | tf_op jit(solution)/shard_map/ppermute | solution.py:54
  5.9 7.1 %collective-permute-start.1 = (bf16[528,128]{1,0:T(8,128)(2,1)S(1)}, bf16[528,128]{1,0:T(8,128)(2,1)S(1)}, u32[]{:S(2)}, u32[]{:S(2)}) collective-permute-start(bf16[528,128]{1,0:T(8,128)(2,1)S(1)} %get-tuple-element.26), channel_id=1, source_target_pairs={{0,16},{4,68},{8,24},{12,76},{16,0},{20,84},{24,8},{28,92},{32,48}... | collective-permute-start | bytes 405512 | tf_op jit(solution)/shard_map/ppermute | solution.py:54
  6.3 6.8 %collective-permute-start = (bf16[528,128]{1,0:T(8,128)(2,1)S(1)}, bf16[528,128]{1,0:T(8,128)(2,1)S(1)}, u32[]{:S(2)}, u32[]{:S(2)}) collective-permute-start(bf16[528,128]{1,0:T(8,128)(2,1)S(1)} %get-tuple-element.26), channel_id=1, source_target_pairs={{0,8},{4,36},{8,16},{12,44},{16,24},{20,52},{24,0},{28,60},{32,40}... | collective-permute-start | bytes 405512 | tf_op jit(solution)/shard_map/ppermute | solution.py:54
  13.1 10.8 %collective-permute-start.6 = (bf16[2112,128]{1,0:T(8,128)(2,1)S(1)}, bf16[2112,128]{1,0:T(8,128)(2,1)S(1)}, u32[]{:S(2)}, u32[]{:S(2)}) collective-permute-start(bf16[2112,128]{1,0:T(8,128)(2,1)S(1)} %constant_dynamic-update-slice_fusion.refs_4_), channel_id=1, source_target_pairs={{0,4},{4,0},{8,12},{12,8},{16,20},{20,16},{24,28},{28,24},{32,36},... | collective-permute-start | bytes 1622024 | tf_op jit(solution)/shard_map/ppermute | solution.py:42
  14.8 19.0 %collective-permute-start.5 = (bf16[2112,128]{1,0:T(8,128)(2,1)S(1)}, bf16[2112,128]{1,0:T(8,128)(2,1)S(1)}, u32[]{:S(2)}, u32[]{:S(2)}) collective-permute-start(bf16[2112,128]{1,0:T(8,128)(2,1)S(1)} %constant_dynamic-update-slice_fusion.refs_4_), channel_id=1, source_target_pairs={{0,96},{4,28},{8,104},{12,4},{16,112},{20,12},{24,120},{28,20},{32... | collective-permute-start | bytes 1622024 | tf_op jit(solution)/shard_map/ppermute | solution.py:54
  15.5 18.3 %collective-permute-start.4 = (bf16[2112,128]{1,0:T(8,128)(2,1)S(1)}, bf16[2112,128]{1,0:T(8,128)(2,1)S(1)}, u32[]{:S(2)}, u32[]{:S(2)}) collective-permute-start(bf16[2112,128]{1,0:T(8,128)(2,1)S(1)} %constant_dynamic-update-slice_fusion.refs_4_), channel_id=1, source_target_pairs={{0,64},{4,20},{8,72},{12,28},{16,80},{20,4},{24,88},{28,12},{32,96... | collective-permute-start | bytes 1622024 | tf_op jit(solution)/shard_map/ppermute | solution.py:54
  16.2 17.6 %collective-permute-start.3 = (bf16[2112,128]{1,0:T(8,128)(2,1)S(1)}, bf16[2112,128]{1,0:T(8,128)(2,1)S(1)}, u32[]{:S(2)}, u32[]{:S(2)}) collective-permute-start(bf16[2112,128]{1,0:T(8,128)(2,1)S(1)} %constant_dynamic-update-slice_fusion.refs_4_), channel_id=1, source_target_pairs={{0,32},{4,12},{8,40},{12,20},{16,48},{20,28},{24,56},{28,4},{32,64... | collective-permute-start | bytes 1622024 | tf_op jit(solution)/shard_map/ppermute | solution.py:54
  33.8 6.4 %collective-permute-start.7 = (bf16[2112,128]{1,0:T(8,128)(2,1)S(1)}, bf16[2112,128]{1,0:T(8,128)(2,1)S(1)}, u32[]{:S(2)}, u32[]{:S(2)}) collective-permute-start(bf16[2112,128]{1,0:T(8,128)(2,1)S(1)} %collective-permute-done.3.refs_5_), channel_id=1, source_target_pairs={{0,4},{4,0},{8,12},{12,8},{16,20},{20,16},{24,28},{28,24},{32,36},... | collective-permute-start | bytes 1622024 | tf_op jit(solution)/shard_map/ppermute | solution.py:42
  38.7 2.3 %collective-permute-start.8 = (bf16[2112,128]{1,0:T(8,128)(2,1)S(1)}, bf16[2112,128]{1,0:T(8,128)(2,1)S(1)}, u32[]{:S(2)}, u32[]{:S(2)}) collective-permute-start(bf16[2112,128]{1,0:T(8,128)(2,1)S(1)} %collective-permute-done.4.refs_6_), channel_id=1, source_target_pairs={{0,4},{4,0},{8,12},{12,8},{16,20},{20,16},{24,28},{28,24},{32,36},... | collective-permute-start | bytes 1622024 | tf_op jit(solution)/shard_map/ppermute | solution.py:42
  38.8 3.0 %collective-permute-start.9 = (bf16[2112,128]{1,0:T(8,128)(2,1)S(1)}, bf16[2112,128]{1,0:T(8,128)(2,1)S(1)}, u32[]{:S(2)}, u32[]{:S(2)}) collective-permute-start(bf16[2112,128]{1,0:T(8,128)(2,1)S(1)} %collective-permute-done.5.refs_7_), channel_id=1, source_target_pairs={{0,4},{4,0},{8,12},{12,8},{16,20},{20,16},{24,28},{28,24},{32,36},... | collective-permute-start | bytes 1622024 | tf_op jit(solution)/shard_map/ppermute | solution.py:42
  68.7 7.7 %collective-permute-start.12 = (f32[16,512]{1,0:T(8,128)S(1)}, f32[16,512]{1,0:T(8,128)S(1)}, u32[]{:S(2)}, u32[]{:S(2)}) collective-permute-start(f32[16,512]{1,0:T(8,128)S(1)} %multiply_add_fusion.2), channel_id=1, source_target_pairs={{0,3},{1,0},{2,1},{3,2},{4,7},{5,4},{6,5},{7,6},{8,11},{9,8},{10,9... | collective-permute-start | bytes 98312 | tf_op jit(solution)/shard_map/ppermute | solution.py:46
  73.2 4.3 %collective-permute-start.11 = (f32[16,512]{1,0:T(8,128)S(1)}, f32[16,512]{1,0:T(8,128)S(1)}, u32[]{:S(2)}, u32[]{:S(2)}) collective-permute-start(f32[16,512]{1,0:T(8,128)S(1)} %multiply_add_fusion.2), channel_id=1, source_target_pairs={{0,2},{1,3},{2,0},{3,1},{4,6},{5,7},{6,4},{7,5},{8,10},{9,11},{10,... | collective-permute-start | bytes 98312 | tf_op jit(solution)/shard_map/ppermute | solution.py:46
  73.2 4.3 %collective-permute-start.10 = (f32[16,512]{1,0:T(8,128)S(1)}, f32[16,512]{1,0:T(8,128)S(1)}, u32[]{:S(2)}, u32[]{:S(2)}) collective-permute-start(f32[16,512]{1,0:T(8,128)S(1)} %multiply_add_fusion.2), channel_id=1, source_target_pairs={{0,1},{1,2},{2,3},{3,0},{4,5},{5,6},{6,7},{7,4},{8,9},{9,10},{10,1... | collective-permute-start | bytes 98312 | tf_op jit(solution)/shard_map/ppermute | solution.py:46
  104.0 13.3 %collective-permute-start.13 = (f32[32,512]{1,0:T(8,128)S(1)}, f32[32,512]{1,0:T(8,128)S(1)}, u32[]{:S(2)}, u32[]{:S(2)}) collective-permute-start(f32[32,512]{1,0:T(8,128)S(1)} %couriers_1.1), channel_id=1, source_target_pairs={{0,4},{4,0},{8,12},{12,8},{16,20},{20,16},{24,28},{28,24},{32,36},... | collective-permute-start | bytes 196616 | tf_op jit(solution)/shard_map/ppermute | solution.py:42
  117.4 3.2 %collective-permute-start.16 = (f32[32,512]{1,0:T(8,128)S(1)}, f32[32,512]{1,0:T(8,128)S(1)}, u32[]{:S(2)}, u32[]{:S(2)}) collective-permute-start(f32[32,512]{1,0:T(8,128)S(1)} %multiply_add_fusion.1), channel_id=1, source_target_pairs={{0,96},{4,28},{8,104},{12,4},{16,112},{20,12},{24,120},{28,20},{32... | collective-permute-start | bytes 196616 | tf_op jit(solution)/shard_map/ppermute | solution.py:54
  117.5 4.7 %collective-permute-start.15 = (f32[32,512]{1,0:T(8,128)S(1)}, f32[32,512]{1,0:T(8,128)S(1)}, u32[]{:S(2)}, u32[]{:S(2)}) collective-permute-start(f32[32,512]{1,0:T(8,128)S(1)} %multiply_add_fusion.1), channel_id=1, source_target_pairs={{0,64},{4,20},{8,72},{12,28},{16,80},{20,4},{24,88},{28,12},{32,96... | collective-permute-start | bytes 196616 | tf_op jit(solution)/shard_map/ppermute | solution.py:54
  117.6 5.7 %collective-permute-start.14 = (f32[32,512]{1,0:T(8,128)S(1)}, f32[32,512]{1,0:T(8,128)S(1)}, u32[]{:S(2)}, u32[]{:S(2)}) collective-permute-start(f32[32,512]{1,0:T(8,128)S(1)} %multiply_add_fusion.1), channel_id=1, source_target_pairs={{0,32},{4,12},{8,40},{12,20},{16,48},{20,28},{24,56},{28,4},{32,64... | collective-permute-start | bytes 196616 | tf_op jit(solution)/shard_map/ppermute | solution.py:54
  123.4 3.2 %collective-permute-start.19 = (f32[32,512]{1,0:T(8,128)S(1)}, f32[32,512]{1,0:T(8,128)S(1)}, u32[]{:S(2)}, u32[]{:S(2)}) collective-permute-start(f32[32,512]{1,0:T(8,128)S(1)} %multiply_add_fusion), channel_id=1, source_target_pairs={{0,24},{4,100},{8,0},{12,108},{16,8},{20,116},{24,16},{28,124},{32... | collective-permute-start | bytes 196616 | tf_op jit(solution)/shard_map/ppermute | solution.py:54
  123.4 4.7 %collective-permute-start.18 = (f32[32,512]{1,0:T(8,128)S(1)}, f32[32,512]{1,0:T(8,128)S(1)}, u32[]{:S(2)}, u32[]{:S(2)}) collective-permute-start(f32[32,512]{1,0:T(8,128)S(1)} %multiply_add_fusion), channel_id=1, source_target_pairs={{0,16},{4,68},{8,24},{12,76},{16,0},{20,84},{24,8},{28,92},{32,48}... | collective-permute-start | bytes 196616 | tf_op jit(solution)/shard_map/ppermute | solution.py:54
  125.4 4.3 %collective-permute-start.17 = (f32[32,512]{1,0:T(8,128)S(1)}, f32[32,512]{1,0:T(8,128)S(1)}, u32[]{:S(2)}, u32[]{:S(2)}) collective-permute-start(f32[32,512]{1,0:T(8,128)S(1)} %multiply_add_fusion), channel_id=1, source_target_pairs={{0,8},{4,36},{8,16},{12,44},{16,24},{20,52},{24,0},{28,60},{32,40}... | collective-permute-start | bytes 196616 | tf_op jit(solution)/shard_map/ppermute | solution.py:54
  156.0 4.9 %collective-permute-start.22 = (f32[16,512]{1,0:T(8,128)S(1)}, f32[16,512]{1,0:T(8,128)S(1)}, u32[]{:S(2)}, u32[]{:S(2)}) collective-permute-start(f32[16,512]{1,0:T(8,128)S(1)} %orders_2.1), channel_id=1, source_target_pairs={{0,3},{1,0},{2,1},{3,2},{4,7},{5,4},{6,5},{7,6},{8,11},{9,8},{10,9... | collective-permute-start | bytes 98312 | tf_op jit(solution)/shard_map/ppermute | solution.py:46
  159.4 4.3 %collective-permute-start.21 = (f32[16,512]{1,0:T(8,128)S(1)}, f32[16,512]{1,0:T(8,128)S(1)}, u32[]{:S(2)}, u32[]{:S(2)}) collective-permute-start(f32[16,512]{1,0:T(8,128)S(1)} %orders_2.1), channel_id=1, source_target_pairs={{0,2},{1,3},{2,0},{3,1},{4,6},{5,7},{6,4},{7,5},{8,10},{9,11},{10,... | collective-permute-start | bytes 98312 | tf_op jit(solution)/shard_map/ppermute | solution.py:46
  160.1 4.0 %collective-permute-start.20 = (f32[16,512]{1,0:T(8,128)S(1)}, f32[16,512]{1,0:T(8,128)S(1)}, u32[]{:S(2)}, u32[]{:S(2)}) collective-permute-start(f32[16,512]{1,0:T(8,128)S(1)} %orders_2.1), channel_id=1, source_target_pairs={{0,1},{1,2},{2,3},{3,0},{4,5},{5,6},{6,7},{7,4},{8,9},{9,10},{10,1... | collective-permute-start | bytes 98312 | tf_op jit(solution)/shard_map/ppermute | solution.py:46
  191.3 34.1 %all-to-all-start = ((f32[32,1,512]{2,1,0:T(1,128)}), f32[32,1,512]{2,1,0:T(1,128)S(1)}, u32[]{:S(2)}, u32[]{:S(2)}) async-start(f32[32,1,512]{2,1,0:T(1,128)} %copy.17), calls=%async_computation | async-start | bytes 131072 | tf_op jit(solution)/shard_map/all_to_all | solution.py:533
  (3 other events, 114.7 us)
